TPU v7x, 32 devices: a whole 2x2x4 slice. The times are simulated.
32 devices in a mesh: dp: 8 (over z, x), seq: 4 (over y, core).
Axes of the slice: x: 2, y: 2, z: 4, core: 2. Of those that a mesh axis runs over, the one named last changes fastest.
Arguments:
- layer_input: bfloat16 [16384, 768], P(('dp', 'seq')), may hold values from -6 to 6
- query_weight: bfloat16 [768, 768], replicated, may hold values from -0.3125 to 0.3125
- query_bias: float32 [768], replicated, may hold values from -3 to 3
- key_weight: bfloat16 [768, 768], replicated, may hold values from -0.3125 to 0.3125
- value_weight: bfloat16 [768, 768], replicated, may hold values from -0.21875 to 0.21875
- value_bias: float32 [768], replicated, may hold values from -3 to 3
- output_weight: bfloat16 [768, 768], replicated, may hold values from -1.25 to 1.25
- output_bias: float32 [768], replicated, may hold values from -1.75 to 1.75
- first_gain: float32 [768], replicated, may hold values from 0.25 to 1.75
- first_shift: float32 [768], replicated, may hold values from -1.75 to 1.75
- up_weight: bfloat16 [768, 3072], replicated, may hold values from -0.21875 to 0.21875
- up_bias: float32 [3072], replicated, may hold values from -3 to 3
- down_weight: bfloat16 [3072, 768], replicated, may hold values from -0.109375 to 0.109375
- down_bias: float32 [768], replicated, may hold values from -1.75 to 1.75
- second_gain: float32 [768], replicated, may hold values from 0.25 to 1.75
- second_shift: float32 [768], replicated, may hold values from -1.75 to 1.75
- out_cotangent: bfloat16 [16384, 768], P(('dp', 'seq')), may hold values from -6 to 6
- passage_lengths: int32 [8, 8], P('dp'), may hold values from 1 to 512, 2048 in all within a row
Outputs:
- layer_output: bfloat16 [16384, 768], P(('dp', 'seq'))
- input_grad: bfloat16 [16384, 768], P(('dp', 'seq'))
- query_weight_grad: float32 [768, 768], P(('dp', 'seq'))
- query_bias_grad: float32 [768], P(('dp', 'seq'))
- key_weight_grad: float32 [768, 768], P(('dp', 'seq'))
- value_weight_grad: float32 [768, 768], P(('dp', 'seq'))
- value_bias_grad: float32 [768], P(('dp', 'seq'))
- output_weight_grad: float32 [768, 768], P(('dp', 'seq'))
- output_bias_grad: float32 [768], P(('dp', 'seq'))
- first_gain_grad: float32 [768], P(('dp', 'seq'))
- first_shift_grad: float32 [768], P(('dp', 'seq'))
- up_weight_grad: float32 [768, 3072], P(('dp', 'seq'))
- up_bias_grad: float32 [3072], P(('dp', 'seq'))
- down_weight_grad: float32 [3072, 768], P(('dp', 'seq'))
- down_bias_grad: float32 [768], P(('dp', 'seq'))
- second_gain_grad: float32 [768], P(('dp', 'seq'))
- second_shift_grad: float32 [768], P(('dp', 'seq'))
Inputs may be any that keep to these rules, and one draw needn't show every extreme that they name: `passage_lengths`: each row lists the passages of one group in order; a row sums to 2048 and its longest passage has exactly 512 tokens.
All inputs are finite; a program needn't handle non-finite values.
Results may differ from a plain program's by a relative error of at most 0.015.
The roundings to bfloat16 on the way count: a program that leaves them out, or rounds other values in their place, can miss the bound.
Values may be sent and summed in bfloat16 or wider, within the bound.
A program may use at most 192 MiB of HBM per device.

v0:
```python
import jax
import jax.numpy as jnp
from jax import lax
from jax.sharding import PartitionSpec as P

HEAD_DIM = 64


layer_eps = 1e-12
masked_score = -1000000000.0


def layer_norm(hidden, gain, shift):
    mean = jnp.mean(hidden, axis=-1, keepdims=True)
    centred = hidden - mean
    variance = jnp.mean(centred * centred, axis=-1, keepdims=True)
    return centred * lax.rsqrt(variance + layer_eps) * gain + shift


def exact_gelu(values):
    return jax.nn.gelu(values, approximate=False)


def segment_ids(lengths_row, count):
    ends = jnp.cumsum(lengths_row)
    positions = jnp.arange(count, dtype=jnp.int32)
    return jnp.sum((positions[:, None] >= ends[None, :]).astype(jnp.int32), axis=1)


def project(inputs, weight):
    return jnp.dot(inputs, weight, preferred_element_type=jnp.float32)


def project_back(grads, weight):
    return lax.dot_general(
        grads, weight, (((1,), (1,)), ((), ())), preferred_element_type=jnp.float32
    )


def weight_grad(inputs, grads):
    return lax.dot_general(
        inputs, grads, (((0,), (0,)), ((), ())), preferred_element_type=jnp.float32
    )


def column_sums(grads):
    return jnp.sum(grads.astype(jnp.float32), axis=0)


def block_scores(query_block, seg_block, key_heads, seg_all, scale):
    raw = jnp.einsum("qhd,khd->hqk", query_block, key_heads, preferred_element_type=jnp.float32)
    same = seg_block[:, None] == seg_all[None, :]
    return jnp.where(same[None], raw * scale, masked_score)


def attend_forward(query_heads, key_heads, value_heads, seg_all, scale, block):
    count, local_heads, head_size = query_heads.shape
    blocks = count // block
    query_blocks = query_heads.reshape(blocks, block, local_heads, head_size)
    seg_blocks = seg_all.reshape(blocks, block)

    def one_block(packed):
        query_block, seg_block = packed
        scores = block_scores(query_block, seg_block, key_heads, seg_all, scale)
        top = jnp.max(scores, axis=-1, keepdims=True)
        weights = jnp.exp(scores - top)
        total = jnp.sum(weights, axis=-1, keepdims=True)
        probs = (weights / total).astype(jnp.bfloat16)
        context = jnp.einsum("hqk,khd->qhd", probs, value_heads, preferred_element_type=jnp.float32)
        return (context.astype(jnp.bfloat16), top + jnp.log(total))

    context, logsum = lax.map(one_block, (query_blocks, seg_blocks))
    return (context.reshape(count, local_heads, head_size), logsum)


def attend_backward(
    query_heads, key_heads, value_heads, seg_all, logsum, context_grad, scale, block
):
    count, local_heads, head_size = query_heads.shape
    blocks = count // block
    stacked = (
        query_heads.reshape(blocks, block, local_heads, head_size),
        seg_all.reshape(blocks, block),
        logsum,
        context_grad.reshape(blocks, block, local_heads, head_size),
    )

    def one_block(carry, packed):
        key_total, value_total = carry
        query_block, seg_block, logsum_block, grad_block = packed
        scores = block_scores(query_block, seg_block, key_heads, seg_all, scale)
        probs = jnp.exp(scores - logsum_block)
        value_total = value_total + jnp.einsum(
            "hqk,qhd->khd",
            probs.astype(jnp.bfloat16),
            grad_block,
            preferred_element_type=jnp.float32,
        )
        prob_grad = jnp.einsum(
            "qhd,khd->hqk", grad_block, value_heads, preferred_element_type=jnp.float32
        )
        delta = jnp.sum(probs * prob_grad, axis=-1, keepdims=True)
        score_grad = (probs * (prob_grad - delta)).astype(jnp.bfloat16)
        query_grad = (
            jnp.einsum("hqk,khd->qhd", score_grad, key_heads, preferred_element_type=jnp.float32)
            * scale
        )
        key_total = (
            key_total
            + jnp.einsum(
                "hqk,qhd->khd", score_grad, query_block, preferred_element_type=jnp.float32
            )
            * scale
        )
        return ((key_total, value_total), query_grad.astype(jnp.bfloat16))

    zeros = jnp.zeros((count, local_heads, head_size), jnp.float32)
    (key_total, value_total), query_grad = lax.scan(one_block, (zeros, zeros), stacked)
    return (
        query_grad.reshape(count, local_heads, head_size),
        key_total.astype(jnp.bfloat16),
        value_total.astype(jnp.bfloat16),
    )


def shards(
    layer_input,
    query_weight,
    query_bias,
    key_weight,
    value_weight,
    value_bias,
    output_weight,
    output_bias,
    first_gain,
    first_shift,
    up_weight,
    up_bias,
    down_weight,
    down_bias,
    second_gain,
    second_shift,
    out_cotangent,
    passage_lengths,
):
    parts = lax.axis_size("seq")
    rows, width = layer_input.shape
    count = rows * parts
    slab = width // parts
    local_heads = slab // HEAD_DIM
    scale = HEAD_DIM ** (-0.5)
    block = min(512, count)
    seg_all = segment_ids(passage_lengths[0], count)

    def qkv_rows():
        queries = (project(layer_input, query_weight) + query_bias).astype(jnp.bfloat16)
        key_rows = project(layer_input, key_weight).astype(jnp.bfloat16)
        value_rows = (project(layer_input, value_weight) + value_bias).astype(jnp.bfloat16)
        return (
            queries.reshape(rows, parts, slab),
            key_rows.reshape(rows, parts, slab),
            value_rows.reshape(rows, parts, slab),
        )

    def heads_layout(received):
        return received.reshape(count, local_heads, HEAD_DIM)

    sent = qkv_rows()
    query_recv, key_recv, value_recv = (
        lax.all_to_all(sent[0], "seq", split_axis=1, concat_axis=0, tiled=True),
        lax.all_to_all(sent[1], "seq", split_axis=1, concat_axis=0, tiled=True),
        lax.all_to_all(sent[2], "seq", split_axis=1, concat_axis=0, tiled=True),
    )
    query_heads = heads_layout(query_recv)
    key_heads = heads_layout(key_recv)
    value_heads = heads_layout(value_recv)
    context_heads, logsum = attend_forward(
        query_heads, key_heads, value_heads, seg_all, scale, block
    )
    context_back = lax.all_to_all(
        context_heads.reshape(count, 1, slab), "seq", split_axis=0, concat_axis=1, tiled=True
    )
    context = context_back.reshape(rows, width)
    attended = project(context, output_weight) + output_bias
    first_sum = layer_input.astype(jnp.float32) + attended
    normed, first_pull = jax.vjp(layer_norm, first_sum, first_gain, first_shift)
    normed_low = normed.astype(jnp.bfloat16)
    up_pre = project(normed_low, up_weight) + up_bias
    activated, gelu_pull = jax.vjp(exact_gelu, up_pre)
    hidden = activated.astype(jnp.bfloat16)
    branch = project(hidden, down_weight) + down_bias
    result, second_pull = jax.vjp(layer_norm, normed + branch, second_gain, second_shift)
    second_grad, second_gain_grad, second_shift_grad = second_pull(
        out_cotangent.astype(jnp.float32)
    )
    branch_grad = second_grad.astype(jnp.bfloat16)
    down_weight_grad = weight_grad(hidden, branch_grad)
    down_bias_grad = column_sums(branch_grad)
    hidden_grad = project_back(branch_grad, down_weight)
    up_grad = gelu_pull(hidden_grad)[0].astype(jnp.bfloat16)
    up_weight_grad = weight_grad(normed_low, up_grad)
    up_bias_grad = column_sums(up_grad)
    normed_grad = project_back(up_grad, up_weight) + second_grad
    first_grad, first_gain_grad, first_shift_grad = first_pull(normed_grad)
    attended_grad = first_grad.astype(jnp.bfloat16)
    output_weight_grad = weight_grad(context, attended_grad)
    output_bias_grad = column_sums(attended_grad)
    context_grad = project_back(attended_grad, output_weight).astype(jnp.bfloat16)
    grad_recv = lax.all_to_all(
        context_grad.reshape(rows, parts, slab), "seq", split_axis=1, concat_axis=0, tiled=True
    )
    resent = qkv_rows()
    query_again, key_again, value_again = (
        lax.all_to_all(resent[0], "seq", split_axis=1, concat_axis=0, tiled=True),
        lax.all_to_all(resent[1], "seq", split_axis=1, concat_axis=0, tiled=True),
        lax.all_to_all(resent[2], "seq", split_axis=1, concat_axis=0, tiled=True),
    )
    query_heads = heads_layout(query_again)
    key_heads = heads_layout(key_again)
    value_heads = heads_layout(value_again)
    query_grad, key_grad, value_grad = attend_backward(
        query_heads, key_heads, value_heads, seg_all, logsum, heads_layout(grad_recv), scale, block
    )
    query_back, key_back, value_back = (
        lax.all_to_all(
            query_grad.reshape(count, 1, slab), "seq", split_axis=0, concat_axis=1, tiled=True
        ),
        lax.all_to_all(
            key_grad.reshape(count, 1, slab), "seq", split_axis=0, concat_axis=1, tiled=True
        ),
        lax.all_to_all(
            value_grad.reshape(count, 1, slab), "seq", split_axis=0, concat_axis=1, tiled=True
        ),
    )
    query_rows_grad = query_back.reshape(rows, width)
    key_rows_grad = key_back.reshape(rows, width)
    value_rows_grad = value_back.reshape(rows, width)
    input_grad = (
        project_back(query_rows_grad, query_weight)
        + project_back(key_rows_grad, key_weight)
        + project_back(value_rows_grad, value_weight)
        + first_grad
    )
    query_weight_grad = weight_grad(layer_input, query_rows_grad)
    query_bias_grad = column_sums(query_rows_grad)
    key_weight_grad = weight_grad(layer_input, key_rows_grad)
    value_weight_grad = weight_grad(layer_input, value_rows_grad)
    value_bias_grad = column_sums(value_rows_grad)
    summed = (
        lax.psum_scatter(query_weight_grad, ("dp", "seq"), scatter_dimension=0, tiled=True),
        lax.psum_scatter(query_bias_grad, ("dp", "seq"), scatter_dimension=0, tiled=True),
        lax.psum_scatter(key_weight_grad, ("dp", "seq"), scatter_dimension=0, tiled=True),
        lax.psum_scatter(value_weight_grad, ("dp", "seq"), scatter_dimension=0, tiled=True),
        lax.psum_scatter(value_bias_grad, ("dp", "seq"), scatter_dimension=0, tiled=True),
        lax.psum_scatter(output_weight_grad, ("dp", "seq"), scatter_dimension=0, tiled=True),
        lax.psum_scatter(output_bias_grad, ("dp", "seq"), scatter_dimension=0, tiled=True),
        lax.psum_scatter(first_gain_grad, ("dp", "seq"), scatter_dimension=0, tiled=True),
        lax.psum_scatter(first_shift_grad, ("dp", "seq"), scatter_dimension=0, tiled=True),
        lax.psum_scatter(up_weight_grad, ("dp", "seq"), scatter_dimension=0, tiled=True),
        lax.psum_scatter(up_bias_grad, ("dp", "seq"), scatter_dimension=0, tiled=True),
        lax.psum_scatter(down_weight_grad, ("dp", "seq"), scatter_dimension=0, tiled=True),
        lax.psum_scatter(down_bias_grad, ("dp", "seq"), scatter_dimension=0, tiled=True),
        lax.psum_scatter(second_gain_grad, ("dp", "seq"), scatter_dimension=0, tiled=True),
        lax.psum_scatter(second_shift_grad, ("dp", "seq"), scatter_dimension=0, tiled=True),
    )
    return (
        result.astype(jnp.bfloat16),
        input_grad.astype(jnp.bfloat16),
        summed[0],
        summed[1],
        summed[2],
        summed[3],
        summed[4],
        summed[5],
        summed[6],
        summed[7],
        summed[8],
        summed[9],
        summed[10],
        summed[11],
        summed[12],
        summed[13],
        summed[14],
    )


def solution(mesh):
    in_specs = (
        P(("dp", "seq"), None),
        P(),
        P(),
        P(),
        P(),
        P(),
        P(),
        P(),
        P(),
        P(),
        P(),
        P(),
        P(),
        P(),
        P(),
        P(),
        P(("dp", "seq"), None),
        P("dp", None),
    )
    out_specs = (
        P(("dp", "seq"), None),
        P(("dp", "seq"), None),
        P(("dp", "seq"), None),
        P(("dp", "seq")),
        P(("dp", "seq"), None),
        P(("dp", "seq"), None),
        P(("dp", "seq")),
        P(("dp", "seq"), None),
        P(("dp", "seq")),
        P(("dp", "seq")),
        P(("dp", "seq")),
        P(("dp", "seq"), None),
        P(("dp", "seq")),
        P(("dp", "seq"), None),
        P(("dp", "seq")),
        P(("dp", "seq")),
        P(("dp", "seq")),
    )
    return jax.shard_map(shards, mesh=mesh, in_specs=in_specs, out_specs=out_specs, check_vma=False)
```

profile of v0, /device:TPU:0, one launch (start us, length us, event | category | flops | bytes accessed | tf_op | source)
XLA Modules:
  0.0 1042.8 jit_solution(3333506981744283167)
XLA Ops:
  18.3 8.4 all-to-all-done.1
  59.0 88.2 %while.27 = (s32[]{:T(128)}, bf16[4,512,3,64]{1,3,2,0:T(8,128)(2,1)}, f32[4,3,512,1]{2,1,3,0:T(4,128)}, s32[4,512]{1,0:T(4,128)}, s32[2048]{0:T(1024)S(1)}, /*in...) while((s32[]{:T(128)}, ...), condition=%wide.region_5.6_spmd, body=%wide.region_2.5_spmd.sunk | while | flops 844200448 | bytes 43975780 | solution.py:72
  66.3 6.8 fusion.131
  73.7 7.3 fusion.132
  88.4 6.8 fusion.131
  95.8 7.3 fusion.132
  117.8 7.3 fusion.132
  139.9 7.3 fusion.132
  162.2 16.3 %all_to_all.135 = bf16[4,2,49152]{2,1,0:T(2,128)(2,1)} all-to-all(bf16[4,2,49152]{2,1,0:T(2,128)(2,1)} %reshape.291), channel_id=1, replica_groups=mesh['dp'=8,'seq'=4] {'seq'}, dimensions={0} | all-to-all | bytes 1572864 | tf_op jit(solution)/shard_map/all_to_all | solution.py:180
  195.5 19.6 %multiply_convert_fusion.1 = (bf16[512,3072]{1,0:T(8,128)(2,1)S(1)}, f32[512,3072]{1,0:T(8,128)}, f32[512,3072]{1,0:T(8,128)}) fusion(f32[3072]{0:T(1024)S(1)} %copy-done.52, bf16[768,3072]{1,0:T(8,128)(2,1)} %param.32, f32[512,768]{1,0:T(8,128)S(1)} %get-tuple-element.333, f32[768]{0:T(1024)S(1)} %copy-done.57, f32[768]{0:T(1024)S(1)} %copy-done.49, ...), kind=kOutput, calls=%fused_computation.56 | convolution fusion | flops 2521694208 | bytes 22042624 | tf_op jit(solution)/shard_map/dot_general | solution.py:31
  222.0 9.8 convert_reduce_fusion
  252.4 7.9 all-to-all-done.4
  261.2 147.2 %while.28 = (s32[]{:T(128)}, f32[2048,3,64]{0,2,1:T(8,128)}, f32[2048,3,64]{0,2,1:T(8,128)}, bf16[4,512,3,64]{1,3,2,0:T(8,128)(2,1)}, bf16[4,512,3,64]{1,3,2,0:T...) while((s32[]{:T(128)}, f32[2048,3,64]{0,2,1:T(8,128)}, ...), condition=%wide.region_16.17_spmd.clone, body=%wide.region_14.16_spmd.clone.sunk | while | flops 2063661568 | bytes 238284784 | solution.py:118
  266.9 6.9 multiply_reduce_fusion.6
  413.9 14.1 %all_to_all.136 = bf16[4,2,49152]{2,1,0:T(2,128)(2,1)S(1)} all-to-all(bf16[4,2,49152]{2,1,0:T(2,128)(2,1)S(1)} %reshape.293), channel_id=1, replica_groups=mesh['dp'=8,'seq'=4] {'seq'}, dimensions={0} | all-to-all | bytes 1572864 | tf_op jit(solution)/shard_map/all_to_all | solution.py:225
  446.7 14.8 %all_to_all.137 = bf16[4,2,49152]{2,1,0:T(2,128)(2,1)} all-to-all(bf16[4,2,49152]{2,1,0:T(2,128)(2,1)S(1)} %reshape.295), channel_id=1, replica_groups=mesh['dp'=8,'seq'=4] {'seq'}, dimensions={0} | all-to-all | bytes 1572864 | tf_op jit(solution)/shard_map/all_to_all | solution.py:228
  479.7 17.8 %all_to_all.138 = bf16[4,2,49152]{2,1,0:T(2,128)(2,1)} all-to-all(bf16[4,2,49152]{2,1,0:T(2,128)(2,1)S(1)} %reshape.297), channel_id=1, replica_groups=mesh['dp'=8,'seq'=4] {'seq'}, dimensions={0} | all-to-all | bytes 1572864 | tf_op jit(solution)/shard_map/all_to_all | solution.py:231
  511.9 9.0 fusion.56
  522.1 8.2 fusion.68
  532.0 41.8 %all-reduce.9 = (f32[768]{0:T(1024)S(1)}, f32[768]{0:T(1024)S(1)}, f32[768]{0:T(1024)S(1)}, f32[768]{0:T(1024)S(1)}, f32[768]{0:T(1024)S(1)}, /*index=5*/f32[307...) all-reduce(f32[768]{0:T(1024)S(1)} %reduce_sum.226, ...), channel_id=3, replica_groups=mesh['dp'=8,'seq'=4] {'dp','seq'}, use_global_device_ids=true, to_apply=%region_19.20.clone | all-reduce | flops 9216 | bytes 73728
  584.3 64.0 %reduce-scatter.21.cloned.1.call-done = f32[24,768]{1,0:T(8,128)} async-done(((f32[768,768]{1,0:T(8,128)}), f32[24,768]{1,0:T(8,128)}) %reduce-scatter.21.cloned.1.call-update) | async-done | bytes 73744
  648.3 104.6 %reduce-scatter.23.cloned.1.call-done = f32[24,768]{1,0:T(8,128)} async-done(((f32[768,768]{1,0:T(8,128)}), f32[24,768]{1,0:T(8,128)}) %reduce-scatter.23.cloned.1.call-update) | async-done | bytes 73744
  752.9 140.8 %reduce-scatter.15.cloned.1.call-done = f32[24,3072]{1,0:T(8,128)} async-done(((f32[768,3072]{1,0:T(8,128)}), f32[24,3072]{1,0:T(8,128)}) %reduce-scatter.15.cloned.1.call-update) | async-done | bytes 294928 | tf_op jit(solution)/shard_map/reduce_scatter | solution.py:259
  893.7 142.0 %reduce-scatter.17.cloned.1.call-done = f32[96,768]{1,0:T(8,128)} async-done(((f32[3072,768]{1,0:T(8,128)}), f32[96,768]{1,0:T(8,128)}) %reduce-scatter.17.cloned.1.call-update) | async-done | bytes 294928 | tf_op jit(solution)/shard_map/reduce_scatter | solution.py:261
  (369 shorter events, 358.0 us)
Async XLA Ops:
  7.2 185.5 %copy-start = (bf16[768,768]{1,0:T(8,128)(2,1)S(1)}, bf16[768,768]{1,0:T(8,128)(2,1)}, u32[]{:S(2)}) copy-start(bf16[768,768]{1,0:T(8,128)(2,1)} %param.28) | copy-start | bytes 3538948
  10.8 15.9 %all-to-all-start.1 = ((bf16[512,4,192]{0,2,1:T(8,128)(2,1)}), bf16[512,4,192]{0,2,1:T(8,128)(2,1)S(1)}, u32[]{:S(2)}, u32[]{:S(2)}) async-start(bf16[512,4,192]{0,2,1:T(8,128)(2,1)} %bitcast.11), calls=%async_computation.1 | async-start | bytes 1572864 | tf_op jit(solution)/shard_map/all_to_all | solution.py:171
  15.1 15.2 %copy-start.54 = (f32[768]{0:T(1024)S(1)}, f32[768]{0:T(1024)}, u32[]{:S(2)}) copy-start(f32[768]{0:T(1024)} %param.24) | copy-start | bytes 9220
  26.7 15.1 %all-to-all-start.2 = ((bf16[512,4,192]{0,2,1:T(8,128)(2,1)}), bf16[512,4,192]{0,2,1:T(8,128)(2,1)S(1)}, u32[]{:S(2)}, u32[]{:S(2)}) async-start(bf16[512,4,192]{0,2,1:T(8,128)(2,1)} %bitcast.192), calls=%async_computation.2 | async-start | bytes 1572864 | tf_op jit(solution)/shard_map/all_to_all | solution.py:172
  30.2 16.2 %copy-start.59 = (s32[1,8]{1,0:T(1,128)S(1)}, s32[1,8]{1,0:T(1,128)}, u32[]{:S(2)}) copy-start(s32[1,8]{1,0:T(1,128)} %param.39) | copy-start | bytes 100
  42.7 15.3 %all-to-all-start = ((bf16[512,4,192]{0,2,1:T(8,128)(2,1)}), bf16[512,4,192]{0,2,1:T(8,128)(2,1)S(1)}, u32[]{:S(2)}, u32[]{:S(2)}) async-start(bf16[512,4,192]{0,2,1:T(8,128)(2,1)} %bitcast.7), calls=%async_computation | async-start | bytes 1572864 | tf_op jit(solution)/shard_map/all_to_all | solution.py:170
  192.7 22.4 %slice-start = ((s8[4718592]{0:T(1024)(128)(4,1)}), s8[4194304]{0:T(1024)(128)(4,1)S(1)}, s32[]{:S(2)}) async-start(s8[4718592]{0:T(1024)(128)(4,1)} %bitcast.206), calls=%async_computation.20 | async-start | bytes 8388608
  195.1 42.5 %copy-start.20 = (f32[512,768]{1,0:T(8,128)}, f32[512,768]{1,0:T(8,128)S(1)}, u32[]{:S(2)}) copy-start(f32[512,768]{1,0:T(8,128)S(1)} %get-tuple-element.333) | copy-start | bytes 4718596
  195.1 42.4 %copy-start.34 = (f32[512]{0:T(512)}, f32[512]{0:T(512)S(1)}, u32[]{:S(2)}) copy-start(f32[512]{0:T(512)S(1)} %broadcast_multiply_fusion.1) | copy-start | bytes 6148
  195.5 42.1 %copy-start.44 = (f32[512]{0:T(512)}, f32[512]{0:T(512)S(1)}, u32[]{:S(2)}) copy-start(f32[512]{0:T(512)S(1)} %fusion.54) | copy-start | bytes 6148
  195.5 19.6 %slice-start.1 = ((s8[4718592]{0:T(1024)(128)(4,1)}), s8[524288]{0:T(1024)(128)(4,1)S(1)}, s32[]{:S(2)}) async-start(s8[4718592]{0:T(1024)(128)(4,1)} %bitcast.206), calls=%async_computation.21 | async-start | bytes 1048576
  195.5 19.6 %copy-start.56 = (f32[768]{0:T(1024)S(1)}, f32[768]{0:T(1024)}, u32[]{:S(2)}) copy-start(f32[768]{0:T(1024)} %param.35) | copy-start | bytes 9220
  219.6 12.2 %slice-start.2 = ((s8[4718592]{0:T(1024)(128)(4,1)}), s8[4194304]{0:T(1024)(128)(4,1)S(1)}, s32[]{:S(2)}) async-start(s8[4718592]{0:T(1024)(128)(4,1)} %bitcast.208), calls=%async_computation.22 | async-start | bytes 8388608
  245.1 15.1 %all-to-all-start.4 = ((bf16[512,4,192]{0,2,1:T(8,128)(2,1)}), bf16[512,4,192]{0,2,1:T(8,128)(2,1)S(1)}, u32[]{:S(2)}, u32[]{:S(2)}) async-start(bf16[512,4,192]{0,2,1:T(8,128)(2,1)} %bitcast.191), calls=%async_computation.4 | async-start | bytes 1572864 | tf_op jit(solution)/shard_map/all_to_all | solution.py:209
  248.6 335.7 %reduce-scatter.13.cloned.1.call-start = ((), (), s32[]{:S(2)}) async-start(), calls=%async_computation.14 | async-start | bytes 2433024 | tf_op jit(solution)/shard_map/reduce_scatter | solution.py:255
  252.3 331.9 %reduce-scatter.19.cloned.1.call-start = ((), (), s32[]{:S(2)}) async-start(), calls=%async_computation.17 | async-start | bytes 2433024
  315.4 12.3 %copy-start.3 = (f32[3,512,2048]{2,1,0:T(8,128)S(1)}, f32[3,512,2048]{2,1,0:T(8,128)}, u32[]{:S(2)}) copy-start(f32[3,512,2048]{2,1,0:T(8,128)} %copy-done.2) | copy-start | bytes 37748740 | tf_op jit(solution)/shard_map/while
  441.5 206.8 %reduce-scatter.21.cloned.1.call-start = ((), (), s32[]{:S(2)}) async-start(), calls=%async_computation.18 | async-start | bytes 2433024
  475.0 277.9 %reduce-scatter.23.cloned.1.call-start = ((), (), s32[]{:S(2)}) async-start(), calls=%async_computation.19 | async-start | bytes 2433024
  511.8 381.9 %reduce-scatter.15.cloned.1.call-start = ((), (), s32[]{:S(2)}) async-start(), calls=%async_computation.15 | async-start | bytes 9732096 | tf_op jit(solution)/shard_map/reduce_scatter | solution.py:259
  520.9 514.8 %reduce-scatter.17.cloned.1.call-start = ((), (), s32[]{:S(2)}) async-start(), calls=%async_computation.16 | async-start | bytes 9732096 | tf_op jit(solution)/shard_map/reduce_scatter | solution.py:261
  530.3 48.8 %copy-start.26 = (bf16[512,4,1,192]{0,3,1,2:T(8,128)(2,1)S(1)}, bf16[512,4,1,192]{0,3,1,2:T(8,128)(2,1)}, u32[]{:S(2)}) copy-start(bf16[512,4,1,192]{0,3,1,2:T(8,128)(2,1)} %copy-done.25) | copy-start | bytes 2359300
  530.4 51.0 %copy-start.28 = (bf16[512,4,1,192]{0,3,1,2:T(8,128)(2,1)S(1)}, bf16[512,4,1,192]{0,3,1,2:T(8,128)(2,1)}, u32[]{:S(2)}) copy-start(bf16[512,4,1,192]{0,3,1,2:T(8,128)(2,1)} %copy-done.27) | copy-start | bytes 2359300
  581.4 454.3 %copy-start.1 = (bf16[768,768]{1,0:T(8,128)(2,1)S(1)}, bf16[768,768]{1,0:T(8,128)(2,1)}, u32[]{:S(2)}) copy-start(bf16[768,768]{1,0:T(8,128)(2,1)} %param.28) | copy-start | bytes 3538948
  (84 other events, 372.2 us)
Sparse Core Ops, SparseCore 0:
  255.3 101.3 reduce-scatter.12
  441.6 102.6 reduce-scatter.18
  550.2 98.0 reduce-scatter.20
  654.9 98.0 reduce-scatter.22
  759.2 134.3 reduce-scatter.14
  901.0 134.6 reduce-scatter.16
where the time goes:
time: 1050 us; the launch traced here: 1040 us
  waiting for transfers between devices  477 us (45%)
  matrix products  241 us (23%)
  local copies, waits for them, and re-layouts  106 us (10%)
  blocking collectives  105 us (10%)
  other arithmetic  82.7 us (8%)
  between operations  15.2 us (1%)
  starting transfers between devices  15.1 us (1%)
    unnamed x9, waiting for transfers between devices  169 us
    reduce_scatter x1, waiting for transfers between devices, shards(): lax.psum_scatter(down_weight_grad, ('dp', 'seq'), scatter_dimension=0, ti...  142 us
    reduce_scatter x1, waiting for transfers between devices, shards(): lax.psum_scatter(up_weight_grad, ('dp', 'seq'), scatter_dimension=0, tile...  141 us
    unnamed x132, local copies, waits for them, and re-layouts  43.5 us
    unnamed x1, blocking collectives  41.8 us
    dot_general x6, matrix products, project(): return jnp.dot(inputs, weight, preferred_element_type=jnp.float32)  32.2 us
    dot_general x8, matrix products, block_scores(): jnp.einsum('qhd,khd->hqk', query_block, key_heads, preferred_element_type...  31.4 us
    dot_general x4, matrix products, one_block(): jnp.einsum('hqk,khd->qhd', probs, value_heads, preferred_element_type=jnp...  29.2 us
  transfers between devices with their start and end apart: 10, of which 8 were waited for; matrix products, arithmetic and copies ran while one was open for 23% of the time, Pallas kernels for 0%

commit v1 on v0

v1 whole, which is shorter than its diff:
```python
import functools

import jax
import jax.numpy as jnp
from jax import lax
from jax.experimental import pallas as pl
from jax.experimental.pallas import tpu as pltpu
from jax.sharding import PartitionSpec as P

HEAD_DIM = 64
PAIR = 2 * HEAD_DIM
AXES = ("dp", "seq")
NEG = -1e30
FLOOR = -3e38
BQ = 256
BK = 256
LEVELS = 5
layer_eps = 1e-12
F32 = jnp.float32
BF16 = jnp.bfloat16


def nn(a, b):
    return lax.dot_general(a, b, (((1,), (0,)), ((), ())), preferred_element_type=F32)


def nt(a, b):
    return lax.dot_general(a, b, (((1,), (1,)), ((), ())), preferred_element_type=F32)


def tn(a, b):
    return lax.dot_general(a, b, (((0,), (0,)), ((), ())), preferred_element_type=F32)


def cost(flops, nbytes, trans=0):
    return pl.CostEstimate(flops=int(flops), bytes_accessed=int(nbytes), transcendentals=int(trans))


def params(limit=56 << 20):
    return pltpu.CompilerParams(vmem_limit_bytes=limit)


def whole():
    return pl.BlockSpec(memory_space=pltpu.VMEM)


def hbm():
    return pl.BlockSpec(memory_space=pl.ANY)


def low_lanes():
    return lax.broadcasted_iota(jnp.int32, (1, PAIR), 1) < HEAD_DIM


def qkv_kernel(x_ref, wq, bq, wk, wv, bv, q_ref, k_ref, v_ref):
    x = x_ref[...]
    q_ref[...] = (nn(x, wq[...]) + bq[...]).astype(BF16)
    k_ref[...] = nn(x, wk[...]).astype(BF16)
    v_ref[...] = (nn(x, wv[...]) + bv[...]).astype(BF16)


def project_qkv(x, wq, bq, wk, wv, bv):
    rows, width = x.shape
    step = 256
    wide = pl.BlockSpec((width, width), lambda i: (0, 0))
    one = pl.BlockSpec((1, width), lambda i: (0, 0))
    tile = pl.BlockSpec((step, width), lambda i: (i, 0))
    out = jax.ShapeDtypeStruct((rows, width), BF16)
    return pl.pallas_call(
        qkv_kernel,
        grid=(rows // step,),
        in_specs=[tile, wide, one, wide, wide, one],
        out_specs=[tile] * 3,
        out_shape=[out] * 3,
        compiler_params=params(),
        cost_estimate=cost(6 * rows * width * width, 6 * width * width + 8 * rows * width),
        name="qkv",
    )(x, wq, bq, wk, wv, bv)


def forward_kernel(
    lo_ref, hi_ref, q_ref, kp, ko, kn, vp, vo, vn, onehot, qmask, ctx_ref, lse_ref, ka, kb, vt
):
    rows = q_ref.shape[0]
    low = low_lanes()
    for part, (kpart, vpart) in enumerate(((kp, vp), (ko, vo), (kn, vn))):
        at = slice(part * rows, (part + 1) * rows)
        key = kpart[...]
        hot = onehot[at, :]
        ka[at, :] = jnp.where(low, key, hot)
        kb[at, :] = jnp.where(low, hot, key)
        vt[:, at] = vpart[...].T
    for i in range(rows // BQ):
        block = rows // BQ + i
        at = slice(i * BQ, (i + 1) * BQ)
        query = q_ref[at, :] * BF16(HEAD_DIM**-0.5)
        mask = qmask[rows + i * BQ : rows + (i + 1) * BQ, :]
        qa = jnp.where(low, query, mask)
        qb = jnp.where(low, mask, query)

        def step(j, carry):
            base = pl.multiple_of(j * BK, BK)
            out = []
            for head, (keys, qh) in enumerate(((ka, qa), (kb, qb))):
                top, total, acc = carry[head]
                scores = nt(keys[pl.ds(base, BK), :], qh)
                new_top = jnp.maximum(top, jnp.max(scores, axis=0, keepdims=True))
                weights = jnp.exp(scores - new_top)
                alpha = jnp.exp(top - new_top)
                total = total * alpha + jnp.sum(weights, axis=0, keepdims=True)
                vals = vt[head * HEAD_DIM : (head + 1) * HEAD_DIM, pl.ds(base, BK)]
                acc = acc * alpha + nn(vals, weights.astype(BF16))
                out.append((new_top, total, acc))
            return tuple(out)

        init = (
            jnp.full((1, BQ), FLOOR, F32),
            jnp.zeros((1, BQ), F32),
            jnp.zeros((HEAD_DIM, BQ), F32),
        )
        result = lax.fori_loop(lo_ref[block], hi_ref[block], step, (init, init))
        parts = [acc / total for _, total, acc in result]
        ctx_ref[at, :] = jnp.concatenate(parts, axis=0).T
        for head, (top, total, _) in enumerate(result):
            lse_ref[0, head : head + 1, at] = top + jnp.log(total)


def attend_forward(lo, hi, q, k, v, kh, vh, onehot, qmask):
    rows, width = q.shape
    pairs = width // PAIR
    own = pl.BlockSpec((rows, PAIR), lambda p, *_: (0, p))
    nxt = pl.BlockSpec((rows, PAIR), lambda p, *_: (1, p))
    seg = pl.BlockSpec((3 * rows, PAIR), lambda p, *_: (0, 0))
    grid = pltpu.PrefetchScalarGridSpec(
        num_scalar_prefetch=2,
        grid=(pairs,),
        in_specs=[own, own, own, nxt, own, own, nxt, seg, seg],
        out_specs=[own, pl.BlockSpec((1, 2, rows), lambda p, *_: (p, 0, 0))],
        scratch_shapes=[
            pltpu.VMEM((3 * rows, PAIR), BF16),
            pltpu.VMEM((3 * rows, PAIR), BF16),
            pltpu.VMEM((PAIR, 3 * rows), BF16),
        ],
    )
    return pl.pallas_call(
        forward_kernel,
        grid_spec=grid,
        out_shape=[
            jax.ShapeDtypeStruct((rows, width), F32),
            jax.ShapeDtypeStruct((pairs, 2, rows), F32),
        ],
        compiler_params=params(),
        cost_estimate=cost(8 * rows * rows * width, 24 * rows * width),
        name="attend_forward",
    )(lo, hi, q, kh, k, kh, vh, v, vh, onehot, qmask)


def backward_kernel(
    lo_ref, hi_ref, qp, qo, qn, kp, ko, kn, vp, vo, vn, gp, go, gn, sp, so, sn, onehot, qmask,
    dq_ref, dk_ref, dv_ref, ka, kb, kt, vs, dk_acc, dv_acc,
):
    rows = qo.shape[0]
    per = rows // BQ
    low = low_lanes()
    zero = jnp.zeros((1, PAIR), BF16)
    for part, (kpart, vpart) in enumerate(((kp, vp), (ko, vo), (kn, vn))):
        at = slice(part * rows, (part + 1) * rows)
        key = kpart[...]
        hot = onehot[at, :]
        ka[at, :] = jnp.where(low, key, hot)
        kb[at, :] = jnp.where(low, hot, key)
        kt[:, at] = key.T
        vs[at, :] = vpart[...]
    dk_acc[...] = jnp.zeros_like(dk_acc)
    dv_acc[...] = jnp.zeros_like(dv_acc)
    for i in range(3 * per):
        part = i // per
        own_q = part == 1
        at = slice((i % per) * BQ, (i % per + 1) * BQ)
        stat = (sp, so, sn)[part]
        query = (qp, qo, qn)[part][at, :] * BF16(HEAD_DIM**-0.5)
        grad = (gp, go, gn)[part][at, :]
        mask = qmask[i * BQ : (i + 1) * BQ, :]
        qs = (jnp.where(low, query, mask), jnp.where(low, mask, query))
        qz = (jnp.where(low, query, zero), jnp.where(low, zero, query))
        gz = (jnp.where(low, grad, zero), jnp.where(low, zero, grad))
        lse = (stat[0, 0:1, at], stat[0, 1:2, at])
        delta = (stat[0, 2:3, at], stat[0, 3:4, at])

        def step(j, carry, own_k):
            base = pl.multiple_of(j * BK, BK)
            out = []
            dv = dk = None
            for head, keys in enumerate((ka, kb)):
                scores = nt(keys[pl.ds(base, BK), :], qs[head])
                probs = jnp.exp(scores - lse[head])
                prob_grad = nt(vs[pl.ds(base, BK), :], gz[head])
                score_grad = (probs * (prob_grad - delta[head])).astype(BF16)
                if own_k:
                    one = nn(probs.astype(BF16), gz[head])
                    two = nn(score_grad, qz[head])
                    dv = one if dv is None else dv + one
                    dk = two if dk is None else dk + two
                if own_q:
                    rows_t = kt[head * HEAD_DIM : (head + 1) * HEAD_DIM, pl.ds(base, BK)]
                    out.append(carry[head] + nn(rows_t, score_grad))
            if own_k:
                to = pl.ds(pl.multiple_of(base - rows, BK), BK)
                dv_acc[to, :] = dv_acc[to, :] + dv
                dk_acc[to, :] = dk_acc[to, :] + dk
            return tuple(out)

        lo, hi = lo_ref[i], hi_ref[i]
        first, last = rows // BK, 2 * rows // BK
        if own_q:
            init = (jnp.zeros((HEAD_DIM, BQ), F32),) * 2
            outer = functools.partial(step, own_k=False)
            inner = functools.partial(step, own_k=True)
            total = lax.fori_loop(lo, jnp.minimum(hi, first), outer, init)
            total = lax.fori_loop(jnp.maximum(lo, first), jnp.minimum(hi, last), inner, total)
            total = lax.fori_loop(jnp.maximum(lo, last), hi, outer, total)
            dq = jnp.concatenate(total, axis=0) * F32(HEAD_DIM**-0.5)
            dq_ref[at, :] = dq.T.astype(BF16)
        else:
            lax.fori_loop(lo, hi, functools.partial(step, own_k=True), ())
    dk_ref[...] = dk_acc[...].astype(BF16)
    dv_ref[...] = dv_acc[...].astype(BF16)


def attend_backward(lo, hi, q, k, v, qh, kh, vh, g, gp, gn, st, stp, stn, onehot, qmask):
    rows, width = q.shape
    pairs = width // PAIR
    own = pl.BlockSpec((rows, PAIR), lambda p, *_: (0, p))
    nxt = pl.BlockSpec((rows, PAIR), lambda p, *_: (1, p))
    seg = pl.BlockSpec((3 * rows, PAIR), lambda p, *_: (0, 0))
    sta = pl.BlockSpec((1, 4, rows), lambda p, *_: (p, 0, 0))
    out = jax.ShapeDtypeStruct((rows, width), BF16)
    grid = pltpu.PrefetchScalarGridSpec(
        num_scalar_prefetch=2,
        grid=(pairs,),
        in_specs=[own, own, nxt] * 3 + [own] * 3 + [sta] * 3 + [seg, seg],
        out_specs=[own] * 3,
        scratch_shapes=[
            pltpu.VMEM((3 * rows, PAIR), BF16),
            pltpu.VMEM((3 * rows, PAIR), BF16),
            pltpu.VMEM((PAIR, 3 * rows), BF16),
            pltpu.VMEM((3 * rows, PAIR), BF16),
            pltpu.VMEM((rows, PAIR), F32),
            pltpu.VMEM((rows, PAIR), F32),
        ],
    )
    return pl.pallas_call(
        backward_kernel,
        grid_spec=grid,
        out_shape=[out] * 3,
        compiler_params=params(),
        cost_estimate=cost(24 * rows * rows * width, 40 * rows * width),
        name="attend_backward",
    )(lo, hi, qh, q, qh, kh, k, kh, vh, v, vh, gp, g, gn, stp, st, stn, onehot, qmask)


def norm_forward(h):
    mean = jnp.mean(h, axis=-1, keepdims=True)
    centred = h - mean
    variance = jnp.mean(centred * centred, axis=-1, keepdims=True)
    inverse = lax.rsqrt(variance + layer_eps)
    return centred * inverse, inverse


def norm_backward(grad, gain, hat, inverse):
    g = grad * gain
    return inverse * (
        g - jnp.mean(g, axis=-1, keepdims=True) - hat * jnp.mean(g * hat, axis=-1, keepdims=True)
    )


def colsum(v):
    return jnp.sum(v, axis=0, keepdims=True)


def middle_kernel(
    x_ref, ctx_ref, ct_ref, wo, bo, g1, s1, wup_hbm, bup, wdn_hbm, bdn, g2, s2, lse_ref,
    result_ref, fg_ref, ag_ref, cg_ref, hid_ref, ug_ref, nl_ref, bg_ref, cl_ref, stat_ref,
    vec_ref, bup_ref,
    wup, wdn, slope, normed, hat, inv, acc, sems,
):
    rows, width = x_ref.shape
    ff = wup.shape[1]
    rc, fc = 256, 512
    chunks, tiles = rows // rc, ff // fc
    up_copy = pltpu.make_async_copy(wup_hbm, wup, sems.at[0])
    dn_copy = pltpu.make_async_copy(wdn_hbm, wdn, sems.at[1])
    up_copy.start()
    dn_copy.start()

    @pl.loop(0, chunks)
    def _(r):
        at = pl.ds(pl.multiple_of(r * rc, rc), rc)
        c_low = ctx_ref[at, :].astype(BF16)
        cl_ref[at, :] = c_low
        h = x_ref[at, :].astype(F32) + (nn(c_low, wo[...]) + bo[...])
        xhat, inverse = norm_forward(h)
        out = xhat * g1[...] + s1[...]
        hat[at, :] = xhat
        inv[at, :] = inverse
        normed[at, :] = out
        nl_ref[at, :] = out.astype(BF16)

    up_copy.wait()
    dn_copy.wait()
    acc[...] = jnp.zeros_like(acc)

    @pl.loop(0, tiles)
    def _(j):
        cols = pl.ds(pl.multiple_of(j * fc, fc), fc)
        for r in range(chunks):
            at = slice(r * rc, (r + 1) * rc)
            up = nn(nl_ref[at, :], wup[:, cols]) + bup[:, cols]
            cdf = 0.5 * (1.0 + lax.erf(up * F32(0.5**0.5)))
            density = jnp.exp(-0.5 * up * up) * F32(0.3989422804014327)
            slope[at, cols] = cdf + up * density
            act = (up * cdf).astype(BF16)
            hid_ref[at, cols] = act
            acc[at, :] = acc[at, :] + nn(act, wdn[cols, :])

    vec_ref[...] = jnp.zeros_like(vec_ref)

    @pl.loop(0, chunks)
    def _(r):
        at = pl.ds(pl.multiple_of(r * rc, rc), rc)
        xhat, inverse = norm_forward(normed[at, :] + (acc[at, :] + bdn[...]))
        result_ref[at, :] = (xhat * g2[...] + s2[...]).astype(BF16)
        ct = ct_ref[at, :].astype(F32)
        second = norm_backward(ct, g2[...], xhat, inverse)
        low = second.astype(BF16)
        bg_ref[at, :] = low
        acc[at, :] = second
        vec_ref[0:1, :] = vec_ref[0:1, :] + colsum(ct * xhat)
        vec_ref[1:2, :] = vec_ref[1:2, :] + colsum(ct)
        vec_ref[2:3, :] = vec_ref[2:3, :] + colsum(low.astype(F32))

    @pl.loop(0, tiles)
    def _(j):
        cols = pl.ds(pl.multiple_of(j * fc, fc), fc)
        sums = jnp.zeros((1, fc), F32)
        for r in range(chunks):
            at = slice(r * rc, (r + 1) * rc)
            ug = (nt(bg_ref[at, :], wdn[cols, :]) * slope[at, cols]).astype(BF16)
            ug_ref[at, cols] = ug
            sums = sums + colsum(ug.astype(F32))
            acc[at, :] = acc[at, :] + nt(ug, wup[:, cols])
        bup_ref[:, cols] = sums

    for r in range(chunks):
        at = slice(r * rc, (r + 1) * rc)
        total = acc[at, :]
        xhat = hat[at, :]
        first = norm_backward(total, g1[...], xhat, inv[at, :])
        fg_ref[at, :] = first
        low = first.astype(BF16)
        ag_ref[at, :] = low
        vec_ref[3:4, :] = vec_ref[3:4, :] + colsum(total * xhat)
        vec_ref[4:5, :] = vec_ref[4:5, :] + colsum(total)
        vec_ref[5:6, :] = vec_ref[5:6, :] + colsum(low.astype(F32))
        cg = nt(low, wo[...]).astype(BF16)
        cg_ref[at, :] = cg
        prod = cg.astype(F32) * ctx_ref[at, :]
        for p in range(width // PAIR):
            flip = prod[:, p * PAIR : (p + 1) * PAIR].T
            stat_ref[p, 2:3, at] = colsum(flip[:HEAD_DIM])
            stat_ref[p, 3:4, at] = colsum(flip[HEAD_DIM:])
    for p in range(width // PAIR):
        stat_ref[p, 0:2, :] = lse_ref[p]


def middle(x, ctx, ct, wo, bo, g1, s1, wup, bup, wdn, bdn, g2, s2, lse):
    rows, width = x.shape
    ff = wup.shape[1]
    pairs = width // PAIR

    def out(shape, dtype):
        return jax.ShapeDtypeStruct(shape, dtype)

    shapes = [
        out((rows, width), BF16),
        out((rows, width), F32),
        out((rows, width), BF16),
        out((rows, width), BF16),
        out((rows, ff), BF16),
        out((rows, ff), BF16),
        out((rows, width), BF16),
        out((rows, width), BF16),
        out((rows, width), BF16),
        out((pairs, 4, rows), F32),
        out((8, width), F32),
        out((1, ff), F32),
    ]
    return pl.pallas_call(
        middle_kernel,
        in_specs=[whole()] * 7 + [hbm(), whole(), hbm()] + [whole()] * 4,
        out_specs=[whole()] * 12,
        out_shape=shapes,
        scratch_shapes=[
            pltpu.VMEM((width, ff), BF16),
            pltpu.VMEM((ff, width), BF16),
            pltpu.VMEM((rows, ff), F32),
            pltpu.VMEM((rows, width), F32),
            pltpu.VMEM((rows, width), F32),
            pltpu.VMEM((rows, 1), F32),
            pltpu.VMEM((rows, width), F32),
            pltpu.SemaphoreType.DMA((2,)),
        ],
        compiler_params=params(),
        cost_estimate=cost(8 * rows * width * ff + 4 * rows * width * width, 30 << 20),
        name="middle",
    )(x, ctx, ct, wo, bo, g1, s1, wup, bup, wdn, bdn, g2, s2, lse)


def place_bits(me, order):
    bits = [(me // (1 << b)) % 2 for b in range(LEVELS)]

    def position(c):
        at = 0
        for k, b in enumerate(order):
            bit = bits[b]
            if (c >> b) & 1:
                bit = 1 - bit
            at = at + bit * (1 << (LEVELS - 1 - k))
        return at

    return position


def block_number(ndev, sizes):
    me = lax.axis_index("dp") * sizes + lax.axis_index("seq")
    return me // (ndev >> LEVELS)


def ff_grads_kernel(
    ndev, parts, orders, hid, bg, nl, ug, cl, ag, dn_out, up_out, wo_out, dn_s, up_s, wo_s, sems
):
    ff, width = hid.shape[1], bg.shape[1]
    nblk = 1 << LEVELS
    me = block_number(ndev, parts)
    pos = [place_bits(me, o) for o in orders]
    tall, short = ff // nblk, width // nblk
    tile = 4 * tall
    bgv = bg[...]

    @pl.loop(0, ff // tile)
    def _(j):
        grad = tn(hid[:, pl.ds(pl.multiple_of(j * tile, tile), tile)], bgv)
        dn_s[pl.ds(4 * j, 4)] = grad.reshape(4, tall, width).astype(BF16)

    for c in range(nblk):
        pltpu.make_async_copy(dn_s.at[c], dn_out.at[pos[0](c)], sems.at[0]).start()
    fc = 512

    @pl.loop(0, ff // fc)
    def _(j):
        cols = pl.ds(pl.multiple_of(j * fc, fc), fc)
        grad = tn(nl[...], ug[:, cols])
        up_s[:, :, cols] = grad.reshape(nblk, short, fc).astype(BF16)

    for c in range(nblk):
        pltpu.make_async_copy(up_s.at[c], up_out.at[pos[1](c)], sems.at[1]).start()
    wo_s[...] = tn(cl[...], ag[...]).reshape(nblk, short, width).astype(BF16)
    for c in range(nblk):
        pltpu.make_async_copy(wo_s.at[c], wo_out.at[pos[2](c)], sems.at[2]).start()
    pltpu.make_async_copy(dn_s, dn_out, sems.at[0]).wait()
    pltpu.make_async_copy(up_s, up_out, sems.at[1]).wait()
    pltpu.make_async_copy(wo_s, wo_out, sems.at[2]).wait()


def ff_grads(ndev, parts, orders, hid, bg, nl, ug, cl, ag):
    rows, ff = hid.shape
    width = bg.shape[1]
    nblk = 1 << LEVELS
    shapes = [(nblk, ff // nblk, width), (nblk, width // nblk, ff), (nblk, width // nblk, width)]
    return pl.pallas_call(
        functools.partial(ff_grads_kernel, ndev, parts, orders),
        in_specs=[whole()] * 6,
        out_specs=[hbm()] * 3,
        out_shape=[jax.ShapeDtypeStruct(s, BF16) for s in shapes],
        scratch_shapes=[pltpu.VMEM(s, BF16) for s in shapes] + [pltpu.SemaphoreType.DMA((3,))],
        compiler_params=params(),
        cost_estimate=cost(4 * rows * width * ff + 2 * rows * width * width, 20 << 20),
        name="ff_grads",
    )(hid, bg, nl, ug, cl, ag)


def input_kernel(
    ndev, parts, order, x, dq, dk, dv, wq, wk, wv, fg, ig_ref, out, vec_ref, scr, sem
):
    width = x.shape[1]
    nblk = 1 << LEVELS
    pos = place_bits(block_number(ndev, parts), order)
    xv = x[...]
    for n, grad in enumerate((dq, dk, dv)):
        scr[:, n] = tn(xv, grad[...]).reshape(nblk, width // nblk, width).astype(BF16)
    for c in range(nblk):
        pltpu.make_async_copy(scr.at[c], out.at[pos(c)], sem).start()
    ig_ref[...] = (
        nt(dq[...], wq[...]) + nt(dk[...], wk[...]) + nt(dv[...], wv[...]) + fg[...]
    ).astype(BF16)
    vec_ref[...] = jnp.zeros_like(vec_ref)
    vec_ref[0:1, :] = colsum(dq[...].astype(F32))
    vec_ref[1:2, :] = colsum(dv[...].astype(F32))
    pltpu.make_async_copy(scr, out, sem).wait()


def input_side(ndev, parts, order, x, dq, dk, dv, wq, wk, wv, fg):
    rows, width = x.shape
    nblk = 1 << LEVELS
    shape = (nblk, 3, width // nblk, width)
    return pl.pallas_call(
        functools.partial(input_kernel, ndev, parts, order),
        in_specs=[whole()] * 8,
        out_specs=[whole(), hbm(), whole()],
        out_shape=[
            jax.ShapeDtypeStruct((rows, width), BF16),
            jax.ShapeDtypeStruct(shape, BF16),
            jax.ShapeDtypeStruct((8, width), F32),
        ],
        scratch_shapes=[pltpu.VMEM(shape, BF16), pltpu.SemaphoreType.DMA(())],
        compiler_params=params(),
        cost_estimate=cost(12 * rows * width * width, 16 << 20),
        name="input_side",
    )(x, dq, dk, dv, wq, wk, wv, fg)


def halve(arr, order, ndev):
    shift = ndev >> LEVELS
    for k, b in enumerate(order):
        half = arr.shape[0] // 2
        flip = shift << b
        got = lax.ppermute(arr[half:], AXES, [(i, i ^ flip) for i in range(ndev)])
        arr = arr[:half].astype(F32) + got.astype(F32)
        if k < len(order) - 1:
            arr = arr.astype(BF16)
    return arr[0]


def finish(block, ndev):
    rest = ndev >> LEVELS
    if rest == 1:
        return block
    step = 1
    me = lax.axis_index("dp") * lax.axis_size("seq") + lax.axis_index("seq")
    arr = block.reshape(rest, block.shape[0] // rest, block.shape[1])
    flip = rest
    while flip > 1:
        flip //= 2
        bit = (me // flip) % 2
        half = arr.shape[0] // 2
        keep = lax.dynamic_slice_in_dim(arr, bit * half, half, 0)
        send = lax.dynamic_slice_in_dim(arr, (1 - bit) * half, half, 0)
        arr = keep + lax.ppermute(send, AXES, [(i, i ^ flip) for i in range(ndev)])
    return arr[0]


def shards(
    layer_input,
    query_weight,
    query_bias,
    key_weight,
    value_weight,
    value_bias,
    output_weight,
    output_bias,
    first_gain,
    first_shift,
    up_weight,
    up_bias,
    down_weight,
    down_bias,
    second_gain,
    second_shift,
    out_cotangent,
    passage_lengths,
):
    parts = lax.axis_size("seq")
    ndev = parts * lax.axis_size("dp")
    rows, width = layer_input.shape
    ff = up_weight.shape[1]
    count = rows * parts
    place = lax.axis_index("seq")
    ahead = [(i, i + 1) for i in range(parts - 1)]
    back = [(i + 1, i) for i in range(parts - 1)]

    def row(v):
        return v.reshape(1, -1)

    x_prev = lax.ppermute(layer_input, "seq", ahead)
    x_next = lax.ppermute(layer_input, "seq", back)
    q, k, v = project_qkv(
        layer_input, query_weight, row(query_bias), key_weight, value_weight, row(value_bias)
    )
    lengths = passage_lengths[0]
    slots = lengths.shape[0]
    upto = jnp.arange(slots)[:, None] >= jnp.arange(slots)[None, :]
    ends = jnp.sum(jnp.where(upto, lengths[None, :], 0), axis=1)
    start = (place - 1) * rows
    where = start + jnp.arange(3 * rows, dtype=jnp.int32)
    seg = jnp.sum((where[:, None] >= ends[None, :]).astype(jnp.int32), axis=1)
    valid = (where >= 0) & (where < count)
    seg = jnp.where(valid, seg, slots)
    lanes = jnp.arange(PAIR, dtype=jnp.int32) % HEAD_DIM
    match = seg[:, None] == lanes[None, :]
    onehot = jnp.where(match, 1.0, 0.0).astype(BF16)
    qmask = jnp.where(match, 0.0, NEG).astype(BF16)
    heads_at = start + jnp.arange(3 * rows // BQ, dtype=jnp.int32) * BQ
    inside = (heads_at >= 0) & (heads_at < count)
    first_end = jnp.where(ends[None, :] <= heads_at[:, None], ends[None, :], 0)
    lo = jnp.max(first_end, axis=1) - start
    far = heads_at + BQ - 1
    hi = jnp.min(jnp.where(ends[None, :] > far[:, None], ends[None, :], count), axis=1) - start
    own_block = (jnp.arange(3 * rows // BQ) * BQ // rows) == 1
    lo = jnp.where(own_block, jnp.maximum(lo, 0), jnp.maximum(lo, rows))
    hi = jnp.where(own_block, jnp.minimum(hi, 3 * rows), jnp.minimum(hi, 2 * rows))
    lo = (lo // BK).astype(jnp.int32)
    hi = jnp.where(inside, (hi + BK - 1) // BK, 0).astype(jnp.int32)

    qh, kh, vh = project_qkv(
        jnp.concatenate([x_prev, x_next], axis=0),
        query_weight, row(query_bias), key_weight, value_weight, row(value_bias),
    )
    ctx, lse = attend_forward(lo, hi, q, k, v, kh, vh, onehot, qmask)
    result, fg, ag, cg, hid, ug, nl, bg, cl, stat, vec, bup = middle(
        layer_input, ctx, out_cotangent, output_weight, row(output_bias), row(first_gain),
        row(first_shift), up_weight, row(up_bias), down_weight, row(down_bias), row(second_gain),
        row(second_shift), lse,
    )
    g_prev = lax.ppermute(cg, "seq", ahead)
    g_next = lax.ppermute(cg, "seq", back)
    s_prev = lax.ppermute(stat, "seq", ahead)
    s_next = lax.ppermute(stat, "seq", back)
    orders = ((0, 2, 1, 3, 4), (0, 1, 2, 3, 4), (0, 3, 4, 2, 1))
    dn_parts, up_parts, wo_parts = ff_grads(ndev, parts, orders, hid, bg, nl, ug, cl, ag)
    dq, dk, dv = attend_backward(
        lo, hi, q, k, v, qh, kh, vh, cg, g_prev, g_next, stat, s_prev, s_next, onehot, qmask
    )
    in_order = (0, 2, 1, 3, 4)
    input_grad, in_parts, vec_in = input_side(
        ndev, parts, in_order, layer_input, dq, dk, dv, query_weight, key_weight, value_weight, fg
    )
    dn_sum = finish(halve(dn_parts, orders[0], ndev), ndev)
    up_sum = finish(halve(up_parts, orders[1], ndev), ndev)
    wo_sum = finish(halve(wo_parts, orders[2], ndev), ndev)
    in_sum = halve(in_parts, in_order, ndev)
    in_sum = [finish(in_sum[n], ndev) for n in range(3)]

    vectors = [vec_in[0], vec_in[1], vec[5], vec[3], vec[4], bup[0], vec[2], vec[0], vec[1]]
    packed = jnp.concatenate([u.reshape(ndev, -1) for u in vectors], axis=1)
    shared = lax.all_to_all(packed, AXES, split_axis=0, concat_axis=0, tiled=True)
    summed = jnp.sum(shared, axis=0)
    sizes = [u.shape[0] // ndev for u in vectors]
    outs = []
    at = 0
    for size in sizes:
        outs.append(summed[at : at + size])
        at += size
    qb, vb, ob, g1g, s1g, ub, db, g2g, s2g = outs
    return (
        result, input_grad, in_sum[0], qb, in_sum[1], in_sum[2], vb, wo_sum, ob, g1g, s1g,
        up_sum, ub, dn_sum, db, g2g, s2g,
    )


def solution(mesh):
    split = P(AXES, None)
    part = P(AXES)
    in_specs = (split,) + (P(),) * 15 + (split, P("dp", None))
    out_specs = (
        split, split, split, part, split, split, part, split, part, part, part,
        split, part, split, part, part, part,
    )
    return jax.shard_map(shards, mesh=mesh, in_specs=in_specs, out_specs=out_specs, check_vma=False)
```

time: 1050 us -> 331 us (0.32)
  waiting for transfers between devices: 477 us -> 76.2 us
  matrix products: 241 us -> 0 us
  Pallas kernels: 0 us -> 112 us
  blocking collectives: 105 us -> 20.5 us
  local copies, waits for them, and re-layouts: 106 us -> 36.2 us
  other arithmetic: 82.7 us -> 17 us
  starting transfers between devices: 15.1 us -> 67.1 us
  between operations: 15.2 us -> 1.16 us
    reduce_scatter x3 -> x0, waiting for transfers between devices: 283 us -> none  [the longest x1 142 us: shards(): lax.psum_scatter(down_weight_grad, ('dp', 'seq'), scatter_dimension=0, ti...]
    dot_general x46 -> x0, matrix products: 241 us -> none  [the longest x6 32.2 us: project(): return jnp.dot(inputs, weight, preferred_element_type=jnp.float32)]
    unnamed x9 -> x0, waiting for transfers between devices: 169 us -> none
    pallas_call x0 -> x7, Pallas kernels: none -> 112 us  [the longest x1 28.6 us: middle(): pl.pallas_call(middle_kernel, in_specs=[whole()] * 7 + [hbm(), whole(), h...]
    ppermute x0 -> x26, waiting for transfers between devices: none -> 76.2 us  [the longest x20 75 us: halve(): got = lax.ppermute(arr[half:], AXES, [(i, i ^ flip) for i in range(ndev)])]
    ppermute x0 -> x26, starting transfers between devices: none -> 67.1 us  [the longest x20 56.1 us: halve(): got = lax.ppermute(arr[half:], AXES, [(i, i ^ flip) for i in range(ndev)])]
    all_to_all x4 -> x1, blocking collectives: 62.9 us -> 20.5 us  [shards(): lax.all_to_all(packed, AXES, split_axis=0, concat_axis=0, tiled=True)]
    unnamed x132 -> x22, local copies, waits for them, and re-layouts: 43.5 us -> 1.17 us
  transfers between devices with their start and end apart: 10 -> 26, of which waited for: 8 -> 11; matrix products, arithmetic and copies ran while one was open for 23% -> 15% of each run, Pallas kernels for 0% -> 11%
where the time goes in v1:
time: 331 us; the launch traced here: 330 us
  Pallas kernels  112 us (34%)
  waiting for transfers between devices  76.2 us (23%)
  starting transfers between devices  67.1 us (20%)
  local copies, waits for them, and re-layouts  36.2 us (11%)
  blocking collectives  20.5 us (6%)
  other arithmetic  17 us (5%)
    ppermute x20, waiting for transfers between devices, halve(): got = lax.ppermute(arr[half:], AXES, [(i, i ^ flip) for i in range(ndev)])  75 us
    ppermute x20, starting transfers between devices, halve(): got = lax.ppermute(arr[half:], AXES, [(i, i ^ flip) for i in range(ndev)])  56.1 us
    pallas_call x1, Pallas kernels, middle(): pl.pallas_call(middle_kernel, in_specs=[whole()] * 7 + [hbm(), whole(), h...  28.6 us
    pallas_call x1, Pallas kernels, attend_backward(): pl.pallas_call(backward_kernel, grid_spec=grid, out_shape=[out] * 3, comp...  23.9 us
    pallas_call x1, Pallas kernels, attend_forward(): pl.pallas_call(forward_kernel, grid_spec=grid, out_shape=[jax.ShapeDtypeS...  23.9 us
    all_to_all x1, blocking collectives, shards(): lax.all_to_all(packed, AXES, split_axis=0, concat_axis=0, tiled=True)  20.5 us
    pallas_call x1, Pallas kernels, ff_grads(): pl.pallas_call(functools.partial(ff_grads_kernel, ndev, parts, orders), i...  14.4 us
    pallas_call x2, Pallas kernels, project_qkv(): pl.pallas_call(qkv_kernel, grid=(rows // step,), in_specs=[tile, wide, on...  12.7 us
  transfers between devices with their start and end apart: 26, of which 11 were waited for; matrix products, arithmetic and copies ran while one was open for 15% of the time, Pallas kernels for 11%

profile of v1, /device:TPU:0, one launch (start us, length us, event | category | flops | bytes accessed | tf_op | source)
XLA Modules:
  0.0 330.3 jit_solution(12491816377970759083)
XLA Ops:
  2.0 3.1 collective-permute-start
  16.8 5.1 %qkv.2 = (bf16[512,768]{1,0:T(8,128)(2,1)}, bf16[512,768]{1,0:T(8,128)(2,1)}, bf16[512,768]{1,0:T(8,128)(2,1)}) custom-call(bf16[512,768]{1,0:T(8,128)(2,1)} %x.1, bf16[768,768]{1,0:T(8,128)(2,1)} %wq.5, f32[1,768]{1,0:T(1,128)} %reshape.101.bq, bf16[768,768]{1,0:T(8,128)(2,1)} %wk.5, bf16[768,768]{1,0:T(8,128)(2,1)} %wv.5, f32[1,768]{1,0:T(1,128)} %reshape.102.bv), custom_call_target="tpu_custom_call" | custom-call | flops 1811939328 | bytes 6684672 | tf_op jit(solution)/shard_map/qkv/pallas_call | solution.py:69
  24.4 7.5 %qkv.3 = (bf16[1024,768]{1,0:T(8,128)(2,1)}, bf16[1024,768]{1,0:T(8,128)(2,1)}, bf16[1024,768]{1,0:T(8,128)(2,1)}) custom-call(bf16[1024,768]{1,0:T(8,128)(2,1)} %pad_maximum_fusion.x_ref, bf16[768,768]{1,0:T(8,128)(2,1)} %wq.5, f32[1,768]{1,0:T(1,128)} %reshape.101.bq, bf16[768,768]{1,0:T(8,128)(2,1)} %wk.5, bf16[768,768]{1,0:T(8,128)(2,1)} %wv.5, ...), custom_call_target="tpu_custom_call" | custom-call | flops 3623878656 | bytes 9830400 | tf_op jit(solution)/shard_map/qkv/pallas_call | solution.py:69
  31.9 23.9 %attend_forward.1 = (f32[512,768]{1,0:T(8,128)}, f32[6,2,512]{2,1,0:T(2,128)}) custom-call(s32[6]{0:T(128)} %get-tuple-element.99.lo_ref, s32[6]{0:T(128)} %get-tuple-element.98.hi_ref, bf16[512,768]{1,0:T(8,128)(2,1)} %get-tuple-element.46.q_ref.qo, bf16[1024,768]{1,0:T(8,128)(2,1)} %get-tuple-element.47.kp.kn, bf16[512,768]{1,0:T(8,128)(2,1)} %get-tuple-element.48.ko, ...), custom_call_target="tpu_custom_call" | custom-call | flops 1610612736 | bytes 9437184 | tf_op jit(solution)/shard_map/attend_forward/pallas_call | solution.py:145
  55.8 28.6 %middle.1 = (bf16[512,768]{1,0:T(8,128)(2,1)}, f32[512,768]{1,0:T(8,128)}, bf16[512,768]{1,0:T(8,128)(2,1)}, bf16[512,768]{1,0:T(8,128)(2,1)}, bf16[512,3072]{1,...) custom-call(bf16[512,768]{1,0:T(8,128)(2,1)} %x.1, ...), custom_call_target="tpu_custom_call" | custom-call | flops 10871635968 | bytes 31457280 | tf_op jit(solution)/shard_map/middle/pallas_call | solution.py:398
  84.4 14.4 %ff_grads.1 = (bf16[32,96,768]{2,1,0:T(8,128)(2,1)}, bf16[32,24,3072]{2,1,0:T(8,128)(2,1)}, bf16[32,24,768]{2,1,0:T(8,128)(2,1)}) custom-call(bf16[512,3072]{1,0:T(8,128)(2,1)} %get-tuple-element.66.hid, bf16[512,768]{1,0:T(8,128)(2,1)} %get-tuple-element.67.bg, bf16[512,768]{1,0:T(8,128)(2,1)} %get-tuple-element.68.nl, ...), custom_call_target="tpu_custom_call" | custom-call | flops 5435817984 | bytes 20971520 | tf_op jit(solution)/shard_map/ff_grads/pallas_call | solution.py:480
  99.9 6.9 %collective-permute-start.11 = (bf16[16,24,768]{2,1,0:T(8,128)(2,1)S(1)}, bf16[16,24,768]{2,1,0:T(8,128)(2,1)S(1)}, u32[]{:S(2)}, u32[]{:S(2)}) collective-permute-start(bf16[16,24,768]{2,1,0:T(8,128)(2,1)S(1)} %slice.207), channel_id=1, source_target_pairs={{0,1},{1,0},{2,3},{3,2},{4,5},{5,4},{6,7},{7,6},{8,9},{9,8},{10,11... | collective-permute-start | bytes 1769480 | tf_op jit(solution)/shard_map/ppermute | solution.py:537
  110.1 3.3 slice.220
  113.4 9.7 %collective-permute-start.16 = (bf16[16,24,3072]{2,1,0:T(8,128)(2,1)}, bf16[16,24,3072]{2,1,0:T(8,128)(2,1)S(1)}, u32[]{:S(2)}, u32[]{:S(2)}) collective-permute-start(bf16[16,24,3072]{2,1,0:T(8,128)(2,1)} %slice.220), channel_id=1, source_target_pairs={{0,1},{1,0},{2,3},{3,2},{4,5},{5,4},{6,7},{7,6},{8,9},{9,8},{10,11... | collective-permute-start | bytes 7077896 | tf_op jit(solution)/shard_map/ppermute | solution.py:537
  130.6 23.9 %attend_backward.1 = (bf16[512,768]{1,0:T(8,128)(2,1)}, bf16[512,768]{1,0:T(8,128)(2,1)}, bf16[512,768]{1,0:T(8,128)(2,1)}) custom-call(s32[6]{0:T(128)} %get-tuple-element.99.lo_ref, s32[6]{0:T(128)} %get-tuple-element.98.hi_ref, bf16[1024,768]{1,0:T(8,128)(2,1)} %get-tuple-element.54.qp.qn, bf16[512,768]{1,0:T(8,128)(2,1)} %get-tuple-element.46.q_ref.qo, ...), custom_call_target="tpu_custom_call" | custom-call | flops 4831838208 | bytes 15728640 | tf_op jit(solution)/shard_map/attend_backward/pallas_call | solution.py:252
  154.5 8.8 %input_side.1 = (bf16[512,768]{1,0:T(8,128)(2,1)}, bf16[32,3,24,768]{3,2,1,0:T(8,128)(2,1)}, f32[8,768]{1,0:T(8,128)}) custom-call(bf16[512,768]{1,0:T(8,128)(2,1)} %x.1, bf16[512,768]{1,0:T(8,128)(2,1)} %get-tuple-element.57.dq, bf16[512,768]{1,0:T(8,128)(2,1)} %get-tuple-element.58.dk, bf16[512,768]{1,0:T(8,128)(2,1)} %get-tuple-element.59.dv, ...), custom_call_target="tpu_custom_call" | custom-call | flops 3623878656 | bytes 16777216 | tf_op jit(solution)/shard_map/input_side/pallas_call | solution.py:516
  163.3 2.9 slice.184
  166.2 9.8 %collective-permute-start.6 = (bf16[16,3,24,768]{3,2,1,0:T(8,128)(2,1)}, bf16[16,3,24,768]{3,2,1,0:T(8,128)(2,1)}, u32[]{:S(2)}, u32[]{:S(2)}) collective-permute-start(bf16[16,3,24,768]{3,2,1,0:T(8,128)(2,1)} %slice.184), channel_id=1, source_target_pairs={{0,1},{1,0},{2,3},{3,2},{4,5},{5,4},{6,7},{7,6},{8,9},{9,8},{10,11... | collective-permute-start | bytes 5308424 | tf_op jit(solution)/shard_map/ppermute | solution.py:537
  188.1 3.2 slice.231
  191.4 16.4 %collective-permute-start.13 = (bf16[4,24,768]{2,1,0:T(8,128)(2,1)S(1)}, bf16[4,24,768]{2,1,0:T(8,128)(2,1)S(1)}, u32[]{:S(2)}, u32[]{:S(2)}) collective-permute-start(bf16[4,24,768]{2,1,0:T(8,128)(2,1)S(1)} %slice.257), channel_id=1, source_target_pairs={{0,16},{1,17},{2,18},{3,19},{4,20},{5,21},{6,22},{7,23},{8,24},{9,... | collective-permute-start | bytes 442376 | tf_op jit(solution)/shard_map/ppermute | solution.py:537
  209.8 20.5 %all_to_all.9 = f32[32,1,288]{2,1,0:T(1,128)S(1)} all-to-all(f32[32,1,288]{2,1,0:T(1,128)S(1)} %all_to_all.6), channel_id=1, replica_groups=mesh['dp'=8,'seq'=4] {'dp','seq'}, dimensions={0} | all-to-all | bytes 73728 | tf_op jit(solution)/shard_map/all_to_all | solution.py:655
  231.1 2.7 add_convert_fusion.1
  240.7 21.6 %collective-permute-done.15 = bf16[1,24,768]{2,1,0:T(8,128)(2,1)S(1)} collective-permute-done((bf16[1,24,768]{2,1,0:T(8,128)(2,1)S(1)}, bf16[1,24,768]{2,1,0:T(8,128)(2,1)S(1)}, u32[]{:S(2)}, u32[]{:S(2)}) %collective-permute-start.15) | collective-permute-done | bytes 36896 | tf_op jit(solution)/shard_map/ppermute | solution.py:537
  269.0 9.1 %collective-permute-done.8 = bf16[4,3,24,768]{3,2,1,0:T(8,128)(2,1)S(1)} collective-permute-done((bf16[4,3,24,768]{3,2,1,0:T(8,128)(2,1)S(1)}, bf16[4,3,24,768]{3,2,1,0:T(8,128)(2,1)S(1)}, u32[]{:S(2)}, u32[]{:S(2)}) %collective-permute-start.8) | collective-permute-done | bytes 442400 | tf_op jit(solution)/shard_map/ppermute | solution.py:537
  278.3 16.1 %collective-permute-done.22 = bf16[8,96,768]{2,1,0:T(8,128)(2,1)S(1)} collective-permute-done((bf16[8,96,768]{2,1,0:T(8,128)(2,1)S(1)}, bf16[8,96,768]{2,1,0:T(8,128)(2,1)S(1)}, u32[]{:S(2)}, u32[]{:S(2)}) %collective-permute-start.22) | collective-permute-done | bytes 1179680 | tf_op jit(solution)/shard_map/ppermute | solution.py:537
  296.1 8.8 %collective-permute-done.18 = bf16[4,24,3072]{2,1,0:T(8,128)(2,1)S(1)} collective-permute-done((bf16[4,24,3072]{2,1,0:T(8,128)(2,1)S(1)}, bf16[4,24,3072]{2,1,0:T(8,128)(2,1)S(1)}, u32[]{:S(2)}, u32[]{:S(2)}) %collective-permute-start.18) | collective-permute-done | bytes 589856 | tf_op jit(solution)/shard_map/ppermute | solution.py:537
  308.2 8.5 %collective-permute-done.19 = bf16[2,24,3072]{2,1,0:T(8,128)(2,1)S(1)} collective-permute-done((bf16[2,24,3072]{2,1,0:T(8,128)(2,1)S(1)}, bf16[2,24,3072]{2,1,0:T(8,128)(2,1)S(1)}, u32[]{:S(2)}, u32[]{:S(2)}) %collective-permute-start.19) | collective-permute-done | bytes 294944 | tf_op jit(solution)/shard_map/ppermute | solution.py:537
  316.9 3.1 collective-permute-done.24
  321.2 6.8 %collective-permute-done.20 = bf16[1,24,3072]{2,1,0:T(8,128)(2,1)S(1)} collective-permute-done((bf16[1,24,3072]{2,1,0:T(8,128)(2,1)S(1)}, bf16[1,24,3072]{2,1,0:T(8,128)(2,1)S(1)}, u32[]{:S(2)}, u32[]{:S(2)}) %collective-permute-start.20) | collective-permute-done | bytes 147488 | tf_op jit(solution)/shard_map/ppermute | solution.py:537
  (137 shorter events, 64.4 us)
Async XLA Ops:
  0.7 22.5 %collective-permute-start.1 = (bf16[512,768]{1,0:T(8,128)(2,1)}, bf16[512,768]{1,0:T(8,128)(2,1)S(1)}, u32[]{:S(2)}, u32[]{:S(2)}) collective-permute-start(bf16[512,768]{1,0:T(8,128)(2,1)} %x.1), channel_id=1, source_target_pairs={{1,0},{2,1},{3,2},{5,4},{6,5},{7,6},{9,8},{10,9},{11,10},{13,12},{... | collective-permute-start | bytes 2359304 | tf_op jit(solution)/shard_map/ppermute | solution.py:595
  2.0 21.2 %collective-permute-start = (bf16[512,768]{1,0:T(8,128)(2,1)}, bf16[512,768]{1,0:T(8,128)(2,1)S(1)}, u32[]{:S(2)}, u32[]{:S(2)}) collective-permute-start(bf16[512,768]{1,0:T(8,128)(2,1)} %x.1), channel_id=1, source_target_pairs={{0,1},{1,2},{2,3},{4,5},{5,6},{6,7},{8,9},{9,10},{10,11},{12,13},{... | collective-permute-start | bytes 2359304 | tf_op jit(solution)/shard_map/ppermute | solution.py:594
  99.9 25.1 %collective-permute-start.11 = (bf16[16,24,768]{2,1,0:T(8,128)(2,1)S(1)}, bf16[16,24,768]{2,1,0:T(8,128)(2,1)S(1)}, u32[]{:S(2)}, u32[]{:S(2)}) collective-permute-start(bf16[16,24,768]{2,1,0:T(8,128)(2,1)S(1)} %slice.207), channel_id=1, source_target_pairs={{0,1},{1,0},{2,3},{3,2},{4,5},{5,4},{6,7},{7,6},{8,9},{9,8},{10,11... | collective-permute-start | bytes 1769480 | tf_op jit(solution)/shard_map/ppermute | solution.py:537
  106.8 22.6 %collective-permute-start.2 = (bf16[512,768]{1,0:T(8,128)(2,1)S(1)}, bf16[512,768]{1,0:T(8,128)(2,1)S(1)}, u32[]{:S(2)}, u32[]{:S(2)}) collective-permute-start(bf16[512,768]{1,0:T(8,128)(2,1)S(1)} %copy-done.3), channel_id=1, source_target_pairs={{0,1},{1,2},{2,3},{4,5},{5,6},{6,7},{8,9},{9,10},{10,11},{12,13},{... | collective-permute-start | bytes 2359304 | tf_op jit(solution)/shard_map/ppermute | solution.py:634
  108.8 20.6 %collective-permute-start.3 = (bf16[512,768]{1,0:T(8,128)(2,1)S(1)}, bf16[512,768]{1,0:T(8,128)(2,1)S(1)}, u32[]{:S(2)}, u32[]{:S(2)}) collective-permute-start(bf16[512,768]{1,0:T(8,128)(2,1)S(1)} %copy-done.3), channel_id=1, source_target_pairs={{1,0},{2,1},{3,2},{5,4},{6,5},{7,6},{9,8},{10,9},{11,10},{13,12},{... | collective-permute-start | bytes 2359304 | tf_op jit(solution)/shard_map/ppermute | solution.py:635
  113.4 117.6 %collective-permute-start.16 = (bf16[16,24,3072]{2,1,0:T(8,128)(2,1)}, bf16[16,24,3072]{2,1,0:T(8,128)(2,1)S(1)}, u32[]{:S(2)}, u32[]{:S(2)}) collective-permute-start(bf16[16,24,3072]{2,1,0:T(8,128)(2,1)} %slice.220), channel_id=1, source_target_pairs={{0,1},{1,0},{2,3},{3,2},{4,5},{5,4},{6,7},{7,6},{8,9},{9,8},{10,11... | collective-permute-start | bytes 7077896 | tf_op jit(solution)/shard_map/ppermute | solution.py:537
  127.4 64.0 %collective-permute-start.12 = (bf16[8,24,768]{2,1,0:T(8,128)(2,1)S(1)}, bf16[8,24,768]{2,1,0:T(8,128)(2,1)S(1)}, u32[]{:S(2)}, u32[]{:S(2)}) collective-permute-start(bf16[8,24,768]{2,1,0:T(8,128)(2,1)S(1)} %slice.255), channel_id=1, source_target_pairs={{0,8},{1,9},{2,10},{3,11},{4,12},{5,13},{6,14},{7,15},{8,0},{9,1},... | collective-permute-start | bytes 884744 | tf_op jit(solution)/shard_map/ppermute | solution.py:537
  166.2 68.4 %collective-permute-start.6 = (bf16[16,3,24,768]{3,2,1,0:T(8,128)(2,1)}, bf16[16,3,24,768]{3,2,1,0:T(8,128)(2,1)}, u32[]{:S(2)}, u32[]{:S(2)}) collective-permute-start(bf16[16,3,24,768]{3,2,1,0:T(8,128)(2,1)} %slice.184), channel_id=1, source_target_pairs={{0,1},{1,0},{2,3},{3,2},{4,5},{5,4},{6,7},{7,6},{8,9},{9,8},{10,11... | collective-permute-start | bytes 5308424 | tf_op jit(solution)/shard_map/ppermute | solution.py:537
  191.3 71.7 %collective-permute-start.21 = (bf16[16,96,768]{2,1,0:T(8,128)(2,1)}, bf16[16,96,768]{2,1,0:T(8,128)(2,1)}, u32[]{:S(2)}, u32[]{:S(2)}) collective-permute-start(bf16[16,96,768]{2,1,0:T(8,128)(2,1)} %slice.231), channel_id=1, source_target_pairs={{0,1},{1,0},{2,3},{3,2},{4,5},{5,4},{6,7},{7,6},{8,9},{9,8},{10,11... | collective-permute-start | bytes 7077896 | tf_op jit(solution)/shard_map/ppermute | solution.py:537
  191.4 38.9 %collective-permute-start.13 = (bf16[4,24,768]{2,1,0:T(8,128)(2,1)S(1)}, bf16[4,24,768]{2,1,0:T(8,128)(2,1)S(1)}, u32[]{:S(2)}, u32[]{:S(2)}) collective-permute-start(bf16[4,24,768]{2,1,0:T(8,128)(2,1)S(1)} %slice.257), channel_id=1, source_target_pairs={{0,16},{1,17},{2,18},{3,19},{4,20},{5,21},{6,22},{7,23},{8,24},{9,... | collective-permute-start | bytes 442376 | tf_op jit(solution)/shard_map/ppermute | solution.py:537
  230.4 7.5 %collective-permute-start.14 = (bf16[2,24,768]{2,1,0:T(8,128)(2,1)S(1)}, bf16[2,24,768]{2,1,0:T(8,128)(2,1)S(1)}, u32[]{:S(2)}, u32[]{:S(2)}) collective-permute-start(bf16[2,24,768]{2,1,0:T(8,128)(2,1)S(1)} %slice.259), channel_id=1, source_target_pairs={{0,4},{1,5},{2,6},{3,7},{4,0},{5,1},{6,2},{7,3},{8,12},{9,13},{10,... | collective-permute-start | bytes 221192 | tf_op jit(solution)/shard_map/ppermute | solution.py:537
  233.9 34.0 %collective-permute-start.17 = (bf16[8,24,3072]{2,1,0:T(8,128)(2,1)S(1)}, bf16[8,24,3072]{2,1,0:T(8,128)(2,1)S(1)}, u32[]{:S(2)}, u32[]{:S(2)}) collective-permute-start(bf16[8,24,3072]{2,1,0:T(8,128)(2,1)S(1)} %slice.263), channel_id=1, source_target_pairs={{0,2},{1,3},{2,0},{3,1},{4,6},{5,7},{6,4},{7,5},{8,10},{9,11},{10,... | collective-permute-start | bytes 3538952 | tf_op jit(solution)/shard_map/ppermute | solution.py:537
  236.6 30.5 %collective-permute-start.7 = (bf16[8,3,24,768]{3,2,1,0:T(8,128)(2,1)S(1)}, bf16[8,3,24,768]{3,2,1,0:T(8,128)(2,1)S(1)}, u32[]{:S(2)}, u32[]{:S(2)}) collective-permute-start(bf16[8,3,24,768]{3,2,1,0:T(8,128)(2,1)S(1)} %slice.244), channel_id=1, source_target_pairs={{0,4},{1,5},{2,6},{3,7},{4,0},{5,1},{6,2},{7,3},{8,12},{9,13},{10,... | collective-permute-start | bytes 2654216 | tf_op jit(solution)/shard_map/ppermute | solution.py:537
  237.9 24.4 %collective-permute-start.15 = (bf16[1,24,768]{2,1,0:T(8,128)(2,1)S(1)}, bf16[1,24,768]{2,1,0:T(8,128)(2,1)S(1)}, u32[]{:S(2)}, u32[]{:S(2)}) collective-permute-start(bf16[1,24,768]{2,1,0:T(8,128)(2,1)S(1)} %slice.261), channel_id=1, source_target_pairs={{0,2},{1,3},{2,0},{3,1},{4,6},{5,7},{6,4},{7,5},{8,10},{9,11},{10,... | collective-permute-start | bytes 110600 | tf_op jit(solution)/shard_map/ppermute | solution.py:537
  265.5 29.0 %collective-permute-start.22 = (bf16[8,96,768]{2,1,0:T(8,128)(2,1)S(1)}, bf16[8,96,768]{2,1,0:T(8,128)(2,1)S(1)}, u32[]{:S(2)}, u32[]{:S(2)}) collective-permute-start(bf16[8,96,768]{2,1,0:T(8,128)(2,1)S(1)} %slice.271), channel_id=1, source_target_pairs={{0,4},{1,5},{2,6},{3,7},{4,0},{5,1},{6,2},{7,3},{8,12},{9,13},{10,... | collective-permute-start | bytes 3538952 | tf_op jit(solution)/shard_map/ppermute | solution.py:537
  267.3 10.8 %collective-permute-start.8 = (bf16[4,3,24,768]{3,2,1,0:T(8,128)(2,1)S(1)}, bf16[4,3,24,768]{3,2,1,0:T(8,128)(2,1)S(1)}, u32[]{:S(2)}, u32[]{:S(2)}) collective-permute-start(bf16[4,3,24,768]{3,2,1,0:T(8,128)(2,1)S(1)} %slice.246), channel_id=1, source_target_pairs={{0,2},{1,3},{2,0},{3,1},{4,6},{5,7},{6,4},{7,5},{8,10},{9,11},{10,... | collective-permute-start | bytes 1327112 | tf_op jit(solution)/shard_map/ppermute | solution.py:537
  268.3 36.7 %collective-permute-start.18 = (bf16[4,24,3072]{2,1,0:T(8,128)(2,1)S(1)}, bf16[4,24,3072]{2,1,0:T(8,128)(2,1)S(1)}, u32[]{:S(2)}, u32[]{:S(2)}) collective-permute-start(bf16[4,24,3072]{2,1,0:T(8,128)(2,1)S(1)} %slice.265), channel_id=1, source_target_pairs={{0,4},{1,5},{2,6},{3,7},{4,0},{5,1},{6,2},{7,3},{8,12},{9,13},{10,... | collective-permute-start | bytes 1769480 | tf_op jit(solution)/shard_map/ppermute | solution.py:537
  278.2 17.2 %collective-permute-start.9 = (bf16[2,3,24,768]{3,2,1,0:T(8,128)(2,1)S(1)}, bf16[2,3,24,768]{3,2,1,0:T(8,128)(2,1)S(1)}, u32[]{:S(2)}, u32[]{:S(2)}) collective-permute-start(bf16[2,3,24,768]{3,2,1,0:T(8,128)(2,1)S(1)} %slice.248), channel_id=1, source_target_pairs={{0,8},{1,9},{2,10},{3,11},{4,12},{5,13},{6,14},{7,15},{8,0},{9,1},... | collective-permute-start | bytes 663560 | tf_op jit(solution)/shard_map/ppermute | solution.py:537
  294.8 11.1 %collective-permute-start.23 = (bf16[4,96,768]{2,1,0:T(8,128)(2,1)S(1)}, bf16[4,96,768]{2,1,0:T(8,128)(2,1)S(1)}, u32[]{:S(2)}, u32[]{:S(2)}) collective-permute-start(bf16[4,96,768]{2,1,0:T(8,128)(2,1)S(1)} %slice.273), channel_id=1, source_target_pairs={{0,2},{1,3},{2,0},{3,1},{4,6},{5,7},{6,4},{7,5},{8,10},{9,11},{10,... | collective-permute-start | bytes 1769480 | tf_op jit(solution)/shard_map/ppermute | solution.py:537
  295.5 11.9 %collective-permute-start.10 = (bf16[1,3,24,768]{3,2,1,0:T(8,128)(2,1)S(1)}, bf16[1,3,24,768]{3,2,1,0:T(8,128)(2,1)S(1)}, u32[]{:S(2)}, u32[]{:S(2)}) collective-permute-start(bf16[1,3,24,768]{3,2,1,0:T(8,128)(2,1)S(1)} %slice.250), channel_id=1, source_target_pairs={{0,16},{1,17},{2,18},{3,19},{4,20},{5,21},{6,22},{7,23},{8,24},{9,... | collective-permute-start | bytes 331784 | tf_op jit(solution)/shard_map/ppermute | solution.py:537
  305.1 11.6 %collective-permute-start.19 = (bf16[2,24,3072]{2,1,0:T(8,128)(2,1)S(1)}, bf16[2,24,3072]{2,1,0:T(8,128)(2,1)S(1)}, u32[]{:S(2)}, u32[]{:S(2)}) collective-permute-start(bf16[2,24,3072]{2,1,0:T(8,128)(2,1)S(1)} %slice.267), channel_id=1, source_target_pairs={{0,8},{1,9},{2,10},{3,11},{4,12},{5,13},{6,14},{7,15},{8,0},{9,1},... | collective-permute-start | bytes 884744 | tf_op jit(solution)/shard_map/ppermute | solution.py:537
  306.1 13.9 %collective-permute-start.24 = (bf16[2,96,768]{2,1,0:T(8,128)(2,1)S(1)}, bf16[2,96,768]{2,1,0:T(8,128)(2,1)S(1)}, u32[]{:S(2)}, u32[]{:S(2)}) collective-permute-start(bf16[2,96,768]{2,1,0:T(8,128)(2,1)S(1)} %slice.275), channel_id=1, source_target_pairs={{0,8},{1,9},{2,10},{3,11},{4,12},{5,13},{6,14},{7,15},{8,0},{9,1},... | collective-permute-start | bytes 884744 | tf_op jit(solution)/shard_map/ppermute | solution.py:537
  316.8 11.2 %collective-permute-start.20 = (bf16[1,24,3072]{2,1,0:T(8,128)(2,1)S(1)}, bf16[1,24,3072]{2,1,0:T(8,128)(2,1)S(1)}, u32[]{:S(2)}, u32[]{:S(2)}) collective-permute-start(bf16[1,24,3072]{2,1,0:T(8,128)(2,1)S(1)} %slice.269), channel_id=1, source_target_pairs={{0,16},{1,17},{2,18},{3,19},{4,20},{5,21},{6,22},{7,23},{8,24},{9,... | collective-permute-start | bytes 442376 | tf_op jit(solution)/shard_map/ppermute | solution.py:537
  320.1 9.5 %collective-permute-start.25 = (bf16[1,96,768]{2,1,0:T(8,128)(2,1)S(1)}, bf16[1,96,768]{2,1,0:T(8,128)(2,1)S(1)}, u32[]{:S(2)}, u32[]{:S(2)}) collective-permute-start(bf16[1,96,768]{2,1,0:T(8,128)(2,1)S(1)} %slice.277), channel_id=1, source_target_pairs={{0,16},{1,17},{2,18},{3,19},{4,20},{5,21},{6,22},{7,23},{8,24},{9,... | collective-permute-start | bytes 442376 | tf_op jit(solution)/shard_map/ppermute | solution.py:537
  (13 other events, 142.7 us)

commit v2 on v1

--- a/solution.py
+++ b/solution.py
@@ -52,18 +52,22 @@
     return lax.broadcasted_iota(jnp.int32, (1, PAIR), 1) < HEAD_DIM
 
 
+def line(ref):
+    return ref[...].reshape(1, -1)
+
+
 def qkv_kernel(x_ref, wq, bq, wk, wv, bv, q_ref, k_ref, v_ref):
     x = x_ref[...]
-    q_ref[...] = (nn(x, wq[...]) + bq[...]).astype(BF16)
+    q_ref[...] = (nn(x, wq[...]) + line(bq)).astype(BF16)
     k_ref[...] = nn(x, wk[...]).astype(BF16)
-    v_ref[...] = (nn(x, wv[...]) + bv[...]).astype(BF16)
+    v_ref[...] = (nn(x, wv[...]) + line(bv)).astype(BF16)
 
 
 def project_qkv(x, wq, bq, wk, wv, bv):
     rows, width = x.shape
     step = 256
     wide = pl.BlockSpec((width, width), lambda i: (0, 0))
-    one = pl.BlockSpec((1, width), lambda i: (0, 0))
+    one = pl.BlockSpec((width,), lambda i: (0,))
     tile = pl.BlockSpec((step, width), lambda i: (i, 0))
     out = jax.ShapeDtypeStruct((rows, width), BF16)
     return pl.pallas_call(
@@ -150,7 +154,7 @@
             jax.ShapeDtypeStruct((pairs, 2, rows), F32),
         ],
         compiler_params=params(),
-        cost_estimate=cost(8 * rows * rows * width, 24 * rows * width),
+        cost_estimate=cost(40e9, 24 * rows * width),
         name="attend_forward",
     )(lo, hi, q, kh, k, kh, vh, v, vh, onehot, qmask)
 
@@ -254,7 +258,7 @@
         grid_spec=grid,
         out_shape=[out] * 3,
         compiler_params=params(),
-        cost_estimate=cost(24 * rows * rows * width, 40 * rows * width),
+        cost_estimate=cost(50e9, 40 * rows * width),
         name="attend_backward",
     )(lo, hi, qh, q, qh, kh, k, kh, vh, v, vh, gp, g, gn, stp, st, stn, onehot, qmask)
 
@@ -298,9 +302,9 @@
         at = pl.ds(pl.multiple_of(r * rc, rc), rc)
         c_low = ctx_ref[at, :].astype(BF16)
         cl_ref[at, :] = c_low
-        h = x_ref[at, :].astype(F32) + (nn(c_low, wo[...]) + bo[...])
+        h = x_ref[at, :].astype(F32) + (nn(c_low, wo[...]) + line(bo))
         xhat, inverse = norm_forward(h)
-        out = xhat * g1[...] + s1[...]
+        out = xhat * line(g1) + line(s1)
         hat[at, :] = xhat
         inv[at, :] = inverse
         normed[at, :] = out
@@ -315,7 +319,7 @@
         cols = pl.ds(pl.multiple_of(j * fc, fc), fc)
         for r in range(chunks):
             at = slice(r * rc, (r + 1) * rc)
-            up = nn(nl_ref[at, :], wup[:, cols]) + bup[:, cols]
+            up = nn(nl_ref[at, :], wup[:, cols]) + bup[cols].reshape(1, fc)
             cdf = 0.5 * (1.0 + lax.erf(up * F32(0.5**0.5)))
             density = jnp.exp(-0.5 * up * up) * F32(0.3989422804014327)
             slope[at, cols] = cdf + up * density
@@ -328,10 +332,10 @@
     @pl.loop(0, chunks)
     def _(r):
         at = pl.ds(pl.multiple_of(r * rc, rc), rc)
-        xhat, inverse = norm_forward(normed[at, :] + (acc[at, :] + bdn[...]))
-        result_ref[at, :] = (xhat * g2[...] + s2[...]).astype(BF16)
+        xhat, inverse = norm_forward(normed[at, :] + (acc[at, :] + line(bdn)))
+        result_ref[at, :] = (xhat * line(g2) + line(s2)).astype(BF16)
         ct = ct_ref[at, :].astype(F32)
-        second = norm_backward(ct, g2[...], xhat, inverse)
+        second = norm_backward(ct, line(g2), xhat, inverse)
         low = second.astype(BF16)
         bg_ref[at, :] = low
         acc[at, :] = second
@@ -355,7 +359,7 @@
         at = slice(r * rc, (r + 1) * rc)
         total = acc[at, :]
         xhat = hat[at, :]
-        first = norm_backward(total, g1[...], xhat, inv[at, :])
+        first = norm_backward(total, line(g1), xhat, inv[at, :])
         fg_ref[at, :] = first
         low = first.astype(BF16)
         ag_ref[at, :] = low
@@ -465,8 +469,7 @@
     for c in range(nblk):
         pltpu.make_async_copy(up_s.at[c], up_out.at[pos[1](c)], sems.at[1]).start()
     wo_s[...] = tn(cl[...], ag[...]).reshape(nblk, short, width).astype(BF16)
-    for c in range(nblk):
-        pltpu.make_async_copy(wo_s.at[c], wo_out.at[pos[2](c)], sems.at[2]).start()
+    pltpu.make_async_copy(wo_s, wo_out, sems.at[2]).start()
     pltpu.make_async_copy(dn_s, dn_out, sems.at[0]).wait()
     pltpu.make_async_copy(up_s, up_out, sems.at[1]).wait()
     pltpu.make_async_copy(wo_s, wo_out, sems.at[2]).wait()
@@ -489,56 +492,268 @@
     )(hid, bg, nl, ug, cl, ag)
 
 
-def input_kernel(
-    ndev, parts, order, x, dq, dk, dv, wq, wk, wv, fg, ig_ref, out, vec_ref, scr, sem
+def split_place(me, order):
+    def position(c):
+        at = 0
+        for k, b in enumerate(order):
+            mine, its = (me // (1 << b)) % 2, (c // (1 << b)) % 2
+            at = at + (mine + its - 2 * mine * its) * (1 << (LEVELS - 1 - k))
+        return at
+
+    return position
+
+
+DN_ORDER = (0, 2, 1, 3, 4)
+UP_ORDER = (0, 1, 2, 3, 4)
+ONE_ORDER = (0, 2, 1, 3, 4)
+TWO_ORDER = (0, 1, 2, 4, 3)
+EARLY = 2
+
+
+def tail_kernel(
+    ndev, parts,
+    x, dq, dk, dv, wq, wk, wv, fg, dn_keep, dn_got, up_keep, up_got, wo_parts, vec, bup,
+    ig_ref, dn_out, up_out, wo_out, q_out, k_out, v_out, vec_out, bup_out,
+    dn_s, up_s, one_s, two_s, grad_s, vec_s, bup_s,
+    dn_r, up_r, one_r, two_r, vec_r, bup_r,
+    load_sems, send_sems, recv_sems,
 ):
     width = x.shape[1]
     nblk = 1 << LEVELS
-    pos = place_bits(block_number(ndev, parts), order)
+    short = width // nblk
+    shift = ndev >> LEVELS
+    me = lax.axis_index("dp") * parts + lax.axis_index("seq")
+    block = me // shift
+
+    def partner(flip):
+        other = me + (1 - 2 * ((me // flip) % 2)) * flip
+        return (other // parts, other % parts)
+
+    flips = []
+    flip = 1
+    while flip < ndev:
+        flips.append(flip)
+        flip *= 2
+    barrier = pltpu.get_barrier_semaphore()
+    for flip in flips:
+        pl.semaphore_signal(
+            barrier, inc=1, device_id=partner(flip), device_id_type=pl.DeviceIdType.MESH
+        )
+    pl.semaphore_wait(barrier, len(flips))
+
+    used = [0]
+
+    def exchange(src, dst, flip):
+        n = used[0]
+        used[0] += 1
+        copy = pltpu.make_async_remote_copy(
+            src_ref=src, dst_ref=dst, send_sem=send_sems.at[n], recv_sem=recv_sems.at[n],
+            device_id=partner(flip), device_id_type=pl.DeviceIdType.MESH,
+        )
+        copy.start()
+        return copy
+
+    started = []
+
+    class Chain:
+        def __init__(self, buf, recv, order, done):
+            self.buf, self.recv, self.order, self.step = buf, recv, order, done
+            self.base = 0
+            self.copy = None
+
+        def send(self):
+            half = (1 << LEVELS) >> (self.step + 1)
+            self.half = half
+            self.copy = exchange(
+                self.buf.at[pl.ds(half, half)],
+                self.recv.at[pl.ds(self.base, half)],
+                shift << self.order[self.step],
+            )
+            started.append(self.copy)
+
+        def add(self):
+            self.copy.wait_recv()
+            half, base, buf, recv = self.half, self.base, self.buf, self.recv
+            if half > 1:
+
+                @pl.loop(0, half)
+                def _(i):
+                    buf[i] = (buf[i].astype(F32) + recv[base + i].astype(F32)).astype(BF16)
+
+            self.base += half
+            self.step += 1
+            if half > 1:
+                self.send()
+
+        def last(self):
+            at = self.base - 1
+            return self.buf[0].astype(F32) + self.recv[at].astype(F32)
+
+    dn = Chain(dn_s, dn_r, DN_ORDER, EARLY)
+    up = Chain(up_s, up_r, UP_ORDER, EARLY)
+    one = Chain(one_s, one_r, ONE_ORDER, 0)
+    two = Chain(two_s, two_r, TWO_ORDER, 0)
+
+    loads = [
+        pltpu.make_async_copy(keep.at[pl.ds(0, chain.buf.shape[0])], chain.buf, load_sems.at[n])
+        for n, (chain, keep) in enumerate(((dn, dn_keep), (up, up_keep)))
+    ]
+    for load in loads:
+        load.start()
+
+    def begin(chain, load, got):
+        load.wait()
+
+        @pl.loop(0, chain.buf.shape[0])
+        def _(i):
+            chain.buf[i] = (chain.buf[i].astype(F32) + got[i].astype(F32)).astype(BF16)
+
+        chain.send()
+
+    begin(dn, loads[0], dn_got)
+    begin(up, loads[1], up_got)
+
+    vec_s[0] = vec[...]
+    vec_s[0, 6:7, :] = colsum(dq[...].astype(F32))
+    vec_s[0, 7:8, :] = colsum(dv[...].astype(F32))
+    bup_s[0] = bup[...]
+
+    def vector_send(n):
+        a = exchange(vec_s.at[n], vec_r.at[n], flips[n])
+        b = exchange(bup_s.at[n], bup_r.at[n], flips[n])
+        started.extend((a, b))
+        return a, b
+
+    def vector_add(n, copies):
+        for c in copies:
+            c.wait_recv()
+        vec_s[n + 1] = vec_s[n] + vec_r[n]
+        bup_s[n + 1] = bup_s[n] + bup_r[n]
+        return vector_send(n + 1) if n + 1 < len(flips) else None
+
+    vc = vector_send(0)
     xv = x[...]
-    for n, grad in enumerate((dq, dk, dv)):
-        scr[:, n] = tn(xv, grad[...]).reshape(nblk, width // nblk, width).astype(BF16)
-    for c in range(nblk):
-        pltpu.make_async_copy(scr.at[c], out.at[pos(c)], sem).start()
+
+    def place(chain, offset, order):
+        pos = split_place(block, order)
+
+        @pl.loop(0, nblk)
+        def _(c):
+            at = pl.ds(pl.multiple_of(c * short, short), short)
+            chain.buf[pos(c), offset : offset + short, :] = grad_s[at, :].astype(BF16)
+
+    pos_one = split_place(block, ONE_ORDER)
+
+    @pl.loop(0, nblk)
+    def _(c):
+        one_s[pos_one(c), 0:short, :] = wo_parts[c]
+
+    grad_s[...] = tn(xv, dq[...])
+    place(one, short, ONE_ORDER)
+    one.send()
+    grad_s[...] = tn(xv, dk[...])
+    place(two, 0, TWO_ORDER)
+    grad_s[...] = tn(xv, dv[...])
+    place(two, short, TWO_ORDER)
+    two.send()
+    vc = vector_add(0, vc)
+    one.add()
     ig_ref[...] = (
         nt(dq[...], wq[...]) + nt(dk[...], wk[...]) + nt(dv[...], wv[...]) + fg[...]
     ).astype(BF16)
-    vec_ref[...] = jnp.zeros_like(vec_ref)
-    vec_ref[0:1, :] = colsum(dq[...].astype(F32))
-    vec_ref[1:2, :] = colsum(dv[...].astype(F32))
-    pltpu.make_async_copy(scr, out, sem).wait()
-
-
-def input_side(ndev, parts, order, x, dq, dk, dv, wq, wk, wv, fg):
+    two.add()
+    vc = vector_add(1, vc)
+    dn.add()
+    up.add()
+    one.add()
+    two.add()
+    vc = vector_add(2, vc)
+    dn.add()
+    up.add()
+    one.add()
+    two.add()
+    vc = vector_add(3, vc)
+    dn.add()
+    up.add()
+    dn_out[...] = dn.last()
+    up_out[...] = up.last()
+    one.add()
+    two.add()
+    for n in range(4, len(flips)):
+        vc = vector_add(n, vc)
+    one.add()
+    two.add()
+    both = one.last()
+    wo_out[...] = both[:short]
+    q_out[...] = both[short:]
+    both = two.last()
+    k_out[...] = both[:short]
+    v_out[...] = both[short:]
+    vec_out[...] = vec_s[len(flips)]
+    bup_out[...] = bup_s[len(flips)]
+    for c in started:
+        c.wait_send()
+
+
+def tail(ndev, parts, x, dq, dk, dv, wq, wk, wv, fg, dn, dn_got, up, up_got, wo_parts, vec, bup):
     rows, width = x.shape
     nblk = 1 << LEVELS
-    shape = (nblk, 3, width // nblk, width)
+    short = width // nblk
+    left = nblk >> EARLY
+    tall, ff = dn.shape[1], up.shape[2]
+    steps = ndev.bit_length() - 1
+
+    def out(*shape):
+        return jax.ShapeDtypeStruct(shape, F32)
+
+    copies = 2 * (LEVELS - EARLY) + 2 * LEVELS + 2 * steps
     return pl.pallas_call(
-        functools.partial(input_kernel, ndev, parts, order),
-        in_specs=[whole()] * 8,
-        out_specs=[whole(), hbm(), whole()],
+        functools.partial(tail_kernel, ndev, parts),
+        in_specs=[whole()] * 8
+        + [hbm(), whole(), hbm(), whole()]
+        + [whole()] * 3,
+        out_specs=[whole()] * 9,
         out_shape=[
             jax.ShapeDtypeStruct((rows, width), BF16),
-            jax.ShapeDtypeStruct(shape, BF16),
-            jax.ShapeDtypeStruct((8, width), F32),
+            out(tall, width), out(short, ff),
+            out(short, width), out(short, width), out(short, width), out(short, width),
+            out(8, width), out(1, ff),
         ],
-        scratch_shapes=[pltpu.VMEM(shape, BF16), pltpu.SemaphoreType.DMA(())],
-        compiler_params=params(),
-        cost_estimate=cost(12 * rows * width * width, 16 << 20),
-        name="input_side",
-    )(x, dq, dk, dv, wq, wk, wv, fg)
-
-
-def halve(arr, order, ndev):
+        scratch_shapes=[
+            pltpu.VMEM((left, tall, width), BF16),
+            pltpu.VMEM((left, short, ff), BF16),
+            pltpu.VMEM((nblk, 2 * short, width), BF16),
+            pltpu.VMEM((nblk, 2 * short, width), BF16),
+            pltpu.VMEM((width, width), F32),
+            pltpu.VMEM((steps + 1, 8, width), F32),
+            pltpu.VMEM((steps + 1, 1, ff), F32),
+            pltpu.VMEM((left, tall, width), BF16),
+            pltpu.VMEM((left, short, ff), BF16),
+            pltpu.VMEM((nblk, 2 * short, width), BF16),
+            pltpu.VMEM((nblk, 2 * short, width), BF16),
+            pltpu.VMEM((steps, 8, width), F32),
+            pltpu.VMEM((steps, 1, ff), F32),
+            pltpu.SemaphoreType.DMA((2,)),
+            pltpu.SemaphoreType.DMA((copies,)),
+            pltpu.SemaphoreType.DMA((copies,)),
+        ],
+        compiler_params=pltpu.CompilerParams(
+            vmem_limit_bytes=56 << 20, collective_id=0, has_side_effects=True
+        ),
+        cost_estimate=cost(60e9, 16 << 20),
+        name="tail",
+    )(x, dq, dk, dv, wq, wk, wv, fg, dn, dn_got, up, up_got, wo_parts, vec, bup)
+
+
+def first_halves(arr, order, ndev):
     shift = ndev >> LEVELS
-    for k, b in enumerate(order):
+    for k in range(EARLY):
         half = arr.shape[0] // 2
-        flip = shift << b
+        flip = shift << order[k]
         got = lax.ppermute(arr[half:], AXES, [(i, i ^ flip) for i in range(ndev)])
-        arr = arr[:half].astype(F32) + got.astype(F32)
-        if k < len(order) - 1:
-            arr = arr.astype(BF16)
-    return arr[0]
+        if k + 1 == EARLY:
+            return arr, got
+        arr = (arr[:half].astype(F32) + got.astype(F32)).astype(BF16)
 
 
 def finish(block, ndev):
@@ -588,13 +803,10 @@
     ahead = [(i, i + 1) for i in range(parts - 1)]
     back = [(i + 1, i) for i in range(parts - 1)]
 
-    def row(v):
-        return v.reshape(1, -1)
-
     x_prev = lax.ppermute(layer_input, "seq", ahead)
     x_next = lax.ppermute(layer_input, "seq", back)
     q, k, v = project_qkv(
-        layer_input, query_weight, row(query_bias), key_weight, value_weight, row(value_bias)
+        layer_input, query_weight, query_bias, key_weight, value_weight, value_bias
     )
     lengths = passage_lengths[0]
     slots = lengths.shape[0]
@@ -623,44 +835,40 @@
 
     qh, kh, vh = project_qkv(
         jnp.concatenate([x_prev, x_next], axis=0),
-        query_weight, row(query_bias), key_weight, value_weight, row(value_bias),
+        query_weight, query_bias, key_weight, value_weight, value_bias,
     )
     ctx, lse = attend_forward(lo, hi, q, k, v, kh, vh, onehot, qmask)
     result, fg, ag, cg, hid, ug, nl, bg, cl, stat, vec, bup = middle(
-        layer_input, ctx, out_cotangent, output_weight, row(output_bias), row(first_gain),
-        row(first_shift), up_weight, row(up_bias), down_weight, row(down_bias), row(second_gain),
-        row(second_shift), lse,
+        layer_input, ctx, out_cotangent, output_weight, output_bias, first_gain,
+        first_shift, up_weight, up_bias, down_weight, down_bias, second_gain,
+        second_shift, lse,
     )
     g_prev = lax.ppermute(cg, "seq", ahead)
     g_next = lax.ppermute(cg, "seq", back)
     s_prev = lax.ppermute(stat, "seq", ahead)
     s_next = lax.ppermute(stat, "seq", back)
-    orders = ((0, 2, 1, 3, 4), (0, 1, 2, 3, 4), (0, 3, 4, 2, 1))
-    dn_parts, up_parts, wo_parts = ff_grads(ndev, parts, orders, hid, bg, nl, ug, cl, ag)
+    dn_parts, up_parts, wo_parts = ff_grads(
+        ndev, parts, (DN_ORDER, UP_ORDER), hid, bg, nl, ug, cl, ag
+    )
+    dn_keep, dn_got = first_halves(dn_parts, DN_ORDER, ndev)
+    up_keep, up_got = first_halves(up_parts, UP_ORDER, ndev)
     dq, dk, dv = attend_backward(
         lo, hi, q, k, v, qh, kh, vh, cg, g_prev, g_next, stat, s_prev, s_next, onehot, qmask
     )
-    in_order = (0, 2, 1, 3, 4)
-    input_grad, in_parts, vec_in = input_side(
-        ndev, parts, in_order, layer_input, dq, dk, dv, query_weight, key_weight, value_weight, fg
-    )
-    dn_sum = finish(halve(dn_parts, orders[0], ndev), ndev)
-    up_sum = finish(halve(up_parts, orders[1], ndev), ndev)
-    wo_sum = finish(halve(wo_parts, orders[2], ndev), ndev)
-    in_sum = halve(in_parts, in_order, ndev)
-    in_sum = [finish(in_sum[n], ndev) for n in range(3)]
-
-    vectors = [vec_in[0], vec_in[1], vec[5], vec[3], vec[4], bup[0], vec[2], vec[0], vec[1]]
-    packed = jnp.concatenate([u.reshape(ndev, -1) for u in vectors], axis=1)
-    shared = lax.all_to_all(packed, AXES, split_axis=0, concat_axis=0, tiled=True)
-    summed = jnp.sum(shared, axis=0)
-    sizes = [u.shape[0] // ndev for u in vectors]
-    outs = []
-    at = 0
-    for size in sizes:
-        outs.append(summed[at : at + size])
-        at += size
-    qb, vb, ob, g1g, s1g, ub, db, g2g, s2g = outs
+    ig, dn_sum, up_sum, wo_sum, q_sum, k_sum, v_sum, vecs, bups = tail(
+        ndev, parts, layer_input, dq, dk, dv, query_weight, key_weight, value_weight, fg,
+        dn_keep, dn_got, up_keep, up_got, wo_parts, vec, bup,
+    )
+    dn_sum, up_sum, wo_sum, q_sum, k_sum, v_sum = (
+        finish(u, ndev) for u in (dn_sum, up_sum, wo_sum, q_sum, k_sum, v_sum)
+    )
+    me = lax.axis_index("dp") * parts + place
+    mine = width // ndev
+    cut = lax.dynamic_slice(vecs, (0, me * mine), (8, mine))
+    g2g, s2g, db, g1g, s1g, ob, qb, vb = (cut[n] for n in range(8))
+    ub = lax.dynamic_slice(bups, (0, me * (ff // ndev)), (1, ff // ndev))[0]
+    input_grad = ig
+    in_sum = (q_sum, k_sum, v_sum)
     return (
         result, input_grad, in_sum[0], qb, in_sum[1], in_sum[2], vb, wo_sum, ob, g1g, s1g,
         up_sum, ub, dn_sum, db, g2g, s2g,

time: 331 us -> 267 us (0.81)
  Pallas kernels: 112 us -> 210 us
  waiting for transfers between devices: 76.2 us -> 0.03 us
  starting transfers between devices: 67.1 us -> 24.4 us
  blocking collectives: 20.5 us -> 0 us
  local copies, waits for them, and re-layouts: 36.2 us -> 21.7 us
  other arithmetic: 17 us -> 9.69 us
    pallas_call x1, Pallas kernels: 8.78 us -> 84.7 us  [tail(): pl.pallas_call(functools.partial(tail_kernel, ndev, parts), in_specs=[who...]
    ppermute x20 -> x4, waiting for transfers between devices: 75 us -> 0.01 us  [first_halves(): got = lax.ppermute(arr[half:], AXES, [(i, i ^ flip) for i in range(ndev)])]
    ppermute x20 -> x4, starting transfers between devices: 56.1 us -> 9.02 us  [first_halves(): got = lax.ppermute(arr[half:], AXES, [(i, i ^ flip) for i in range(ndev)])]
    all_to_all x1 -> x0, blocking collectives: 20.5 us -> none  [shards(): lax.all_to_all(packed, AXES, split_axis=0, concat_axis=0, tiled=True)]
    pallas_call x1, Pallas kernels: 23.9 us -> 37.4 us  [attend_backward(): pl.pallas_call(backward_kernel, grid_spec=grid, out_shape=[out] * 3, comp...]
    unnamed x22 -> x31, local copies, waits for them, and re-layouts: 1.17 us -> 12.9 us
    reshape x8 -> x0, local copies, waits for them, and re-layouts: 10.1 us -> none  [row(): return v.reshape(1, -1)]
    another operation x9 -> x0, local copies, waits for them, and re-layouts: 9.14 us -> none  [shards(): packed = jnp.concatenate([u.reshape(ndev, -1) for u in vectors], axis=1)]
  transfers between devices with their start and end apart: 26 -> 10, of which waited for: 11 -> 0; matrix products, arithmetic and copies ran while one was open for 15% -> 4% of each run, Pallas kernels for 11% -> 16%
where the time goes in v2:
time: 267 us
  Pallas kernels  210 us (79%)
  starting transfers between devices  24.4 us (9%)
  local copies, waits for them, and re-layouts  21.7 us (8%)
  other arithmetic  9.69 us (4%)
    pallas_call x1, Pallas kernels, tail(): pl.pallas_call(functools.partial(tail_kernel, ndev, parts), in_specs=[who...  84.7 us
    pallas_call x1, Pallas kernels, attend_backward(): pl.pallas_call(backward_kernel, grid_spec=grid, out_shape=[out] * 3, comp...  37.4 us
    pallas_call x1, Pallas kernels, attend_forward(): pl.pallas_call(forward_kernel, grid_spec=grid, out_shape=[jax.ShapeDtypeS...  32.4 us
    pallas_call x1, Pallas kernels, middle(): pl.pallas_call(middle_kernel, in_specs=[whole()] * 7 + [hbm(), whole(), h...  28.6 us
    pallas_call x1, Pallas kernels, ff_grads(): pl.pallas_call(functools.partial(ff_grads_kernel, ndev, parts, orders), i...  14.4 us
    unnamed x31, local copies, waits for them, and re-layouts  12.9 us
    pallas_call x2, Pallas kernels, project_qkv(): pl.pallas_call(qkv_kernel, grid=(rows // step,), in_specs=[tile, wide, on...  12.7 us
    ppermute x4, starting transfers between devices, first_halves(): got = lax.ppermute(arr[half:], AXES, [(i, i ^ flip) for i in range(ndev)])  9.02 us
  transfers between devices with their start and end apart: 10, of which 0 were waited for; matrix products, arithmetic and copies ran while one was open for 4% of the time, Pallas kernels for 16%

profile of v2, /device:TPU:0, one launch (start us, length us, event | category | flops | bytes accessed | tf_op | source)
XLA Modules:
  0.0 267.0 jit_solution(6725488706556149812)
XLA Ops:
  0.7 1.3 collective-permute-start.1
  2.0 3.1 %collective-permute-start = (bf16[512,768]{1,0:T(8,128)(2,1)}, bf16[512,768]{1,0:T(8,128)(2,1)S(1)}, u32[]{:S(2)}, u32[]{:S(2)}) collective-permute-start(bf16[512,768]{1,0:T(8,128)(2,1)} %x.1), channel_id=1, source_target_pairs={{0,1},{1,2},{2,3},{4,5},{5,6},{6,7},{8,9},{9,10},{10,11},{12,13},{... | collective-permute-start | bytes 2359304 | tf_op jit(solution)/shard_map/ppermute | solution.py:806
  6.7 5.2 %qkv.2 = (bf16[512,768]{1,0:T(8,128)(2,1)}, bf16[512,768]{1,0:T(8,128)(2,1)}, bf16[512,768]{1,0:T(8,128)(2,1)}) custom-call(bf16[512,768]{1,0:T(8,128)(2,1)} %x.1, bf16[768,768]{1,0:T(8,128)(2,1)} %wq.5, f32[768]{0:T(1024)} %bq.3, bf16[768,768]{1,0:T(8,128)(2,1)} %wk.5, bf16[768,768]{1,0:T(8,128)(2,1)} %wv.5, f32[768]{0:T(1024)} %bv.3), custom_call_target="tpu_custom_call" | custom-call | flops 1811939328 | bytes 6684672 | tf_op jit(solution)/shard_map/qkv/pallas_call | solution.py:73
  14.4 7.5 %qkv.3 = (bf16[1024,768]{1,0:T(8,128)(2,1)}, bf16[1024,768]{1,0:T(8,128)(2,1)}, bf16[1024,768]{1,0:T(8,128)(2,1)}) custom-call(bf16[1024,768]{1,0:T(8,128)(2,1)} %pad_maximum_fusion.x_ref, bf16[768,768]{1,0:T(8,128)(2,1)} %wq.5, f32[768]{0:T(1024)} %bq.3, bf16[768,768]{1,0:T(8,128)(2,1)} %wk.5, bf16[768,768]{1,0:T(8,128)(2,1)} %wv.5, f32[768]{0:T(1024)} %bv.3), custom_call_target="tpu_custom_call" | custom-call | flops 3623878656 | bytes 9830400 | tf_op jit(solution)/shard_map/qkv/pallas_call | solution.py:73
  21.9 32.4 %attend_forward.1 = (f32[512,768]{1,0:T(8,128)}, f32[6,2,512]{2,1,0:T(2,128)}) custom-call(s32[6]{0:T(128)} %get-tuple-element.100.lo_ref, s32[6]{0:T(128)} %get-tuple-element.99.hi_ref, bf16[512,768]{1,0:T(8,128)(2,1)} %get-tuple-element.52.q_ref.qo, bf16[1024,768]{1,0:T(8,128)(2,1)} %get-tuple-element.53.kp.kn, bf16[512,768]{1,0:T(8,128)(2,1)} %get-tuple-element.54.ko, ...), custom_call_target="tpu_custom_call" | custom-call | flops 40000000000 | bytes 9437184 | tf_op jit(solution)/shard_map/attend_forward/pallas_call | solution.py:149
  54.3 28.6 %middle.1 = (bf16[512,768]{1,0:T(8,128)(2,1)}, f32[512,768]{1,0:T(8,128)}, bf16[512,768]{1,0:T(8,128)(2,1)}, bf16[512,768]{1,0:T(8,128)(2,1)}, bf16[512,3072]{1,...) custom-call(bf16[512,768]{1,0:T(8,128)(2,1)} %x.1, ...), custom_call_target="tpu_custom_call" | custom-call | flops 10871635968 | bytes 31457280 | tf_op jit(solution)/shard_map/middle/pallas_call | solution.py:402
  82.9 14.4 %ff_grads.1 = (bf16[32,96,768]{2,1,0:T(8,128)(2,1)}, bf16[32,24,3072]{2,1,0:T(8,128)(2,1)}, bf16[32,24,768]{2,1,0:T(8,128)(2,1)}) custom-call(bf16[512,3072]{1,0:T(8,128)(2,1)} %get-tuple-element.67.hid, bf16[512,768]{1,0:T(8,128)(2,1)} %get-tuple-element.68.bg, bf16[512,768]{1,0:T(8,128)(2,1)} %get-tuple-element.69.nl, ...), custom_call_target="tpu_custom_call" | custom-call | flops 5435817984 | bytes 20971520 | tf_op jit(solution)/shard_map/ff_grads/pallas_call | solution.py:483
  97.3 3.4 %slice.46 = bf16[16,24,3072]{2,1,0:T(8,128)(2,1)} slice(bf16[32,24,3072]{2,1,0:T(8,128)(2,1)} %get-tuple-element.74), slice={[16:32], [0:24], [0:3072]} | slice | bytes 4718592 | tf_op jit(solution)/shard_map/slice | solution.py:753
  100.6 8.0 %collective-permute-start.8 = (bf16[16,24,3072]{2,1,0:T(8,128)(2,1)}, bf16[16,24,3072]{2,1,0:T(8,128)(2,1)}, u32[]{:S(2)}, u32[]{:S(2)}) collective-permute-start(bf16[16,24,3072]{2,1,0:T(8,128)(2,1)} %slice.46), channel_id=1, source_target_pairs={{0,1},{1,0},{2,3},{3,2},{4,5},{5,4},{6,7},{7,6},{8,9},{9,8},{10,11... | collective-permute-start | bytes 7077896 | tf_op jit(solution)/shard_map/ppermute | solution.py:753
  108.7 1.5 slice.43
  110.2 1.3 collective-permute-start.5
  111.5 3.0 %collective-permute-start.4 = (f32[6,4,512]{2,1,0:T(4,128)S(1)}, f32[6,4,512]{2,1,0:T(4,128)S(1)}, u32[]{:S(2)}, u32[]{:S(2)}) collective-permute-start(f32[6,4,512]{2,1,0:T(4,128)S(1)} %copy-done.7), channel_id=1, source_target_pairs={{0,1},{1,2},{2,3},{4,5},{5,6},{6,7},{8,9},{9,10},{10,11},{12,13},{... | collective-permute-start | bytes 147464 | tf_op jit(solution)/shard_map/ppermute | solution.py:848
  114.6 1.6 collective-permute-start.3
  116.1 5.2 %collective-permute-start.2 = (bf16[512,768]{1,0:T(8,128)(2,1)}, bf16[512,768]{1,0:T(8,128)(2,1)}, u32[]{:S(2)}, u32[]{:S(2)}) collective-permute-start(bf16[512,768]{1,0:T(8,128)(2,1)} %get-tuple-element.61.go), channel_id=1, source_target_pairs={{0,1},{1,2},{2,3},{4,5},{5,6},{6,7},{8,9},{9,10},{10,11},{12,13},{... | collective-permute-start | bytes 2359304 | tf_op jit(solution)/shard_map/ppermute | solution.py:846
  121.3 3.3 %add_convert_fusion.up_keep = bf16[16,24,3072]{2,1,0:T(8,128)(2,1)S(1)} fusion(bf16[16,24,3072]{2,1,0:T(8,128)(2,1)} %collective-permute-done.8, bf16[32,24,3072]{2,1,0:T(8,128)(2,1)} %get-tuple-element.74), kind=kLoop, calls=%fused_computation | loop fusion | flops 4718592 | bytes 7077888 | tf_op jit(solution)/shard_map/convert_element_type | solution.py:756
  125.8 1.5 copy-done.3
  128.2 2.3 add_convert_fusion.1.dn_keep
  131.6 37.4 %attend_backward.1 = (bf16[512,768]{1,0:T(8,128)(2,1)}, bf16[512,768]{1,0:T(8,128)(2,1)}, bf16[512,768]{1,0:T(8,128)(2,1)}) custom-call(s32[6]{0:T(128)} %get-tuple-element.100.lo_ref, s32[6]{0:T(128)} %get-tuple-element.99.hi_ref, bf16[1024,768]{1,0:T(8,128)(2,1)} %get-tuple-element.60.qp.qn, bf16[512,768]{1,0:T(8,128)(2,1)} %get-tuple-element.52.q_ref.qo, ...), custom_call_target="tpu_custom_call" | custom-call | flops 49999998976 | bytes 15728640 | tf_op jit(solution)/shard_map/attend_backward/pallas_call | solution.py:256
  170.1 84.7 %tail.1 = (bf16[512,768]{1,0:T(8,128)(2,1)}, f32[96,768]{1,0:T(8,128)}, f32[24,3072]{1,0:T(8,128)}, f32[24,768]{1,0:T(8,128)}, f32[24,768]{1,0:T(8,128)}, /*inde...) custom-call(bf16[512,768]{1,0:T(8,128)(2,1)} %x.1, ...), custom_call_target="tpu_custom_call" | custom-call | flops 60000002048 | bytes 16777216 | tf_op jit(solution)/shard_map/tail/pallas_call | solution.py:710
  257.4 2.1 copy.42
  259.5 1.5 copy.43
  261.0 1.5 copy.44
  262.5 1.5 copy.45
  264.1 1.5 copy.46
  (55 shorter events, 12.3 us)
Async XLA Ops:
  0.7 12.4 %collective-permute-start.1 = (bf16[512,768]{1,0:T(8,128)(2,1)}, bf16[512,768]{1,0:T(8,128)(2,1)S(1)}, u32[]{:S(2)}, u32[]{:S(2)}) collective-permute-start(bf16[512,768]{1,0:T(8,128)(2,1)} %x.1), channel_id=1, source_target_pairs={{1,0},{2,1},{3,2},{5,4},{6,5},{7,6},{9,8},{10,9},{11,10},{13,12},{... | collective-permute-start | bytes 2359304 | tf_op jit(solution)/shard_map/ppermute | solution.py:807
  2.0 11.1 %collective-permute-start = (bf16[512,768]{1,0:T(8,128)(2,1)}, bf16[512,768]{1,0:T(8,128)(2,1)S(1)}, u32[]{:S(2)}, u32[]{:S(2)}) collective-permute-start(bf16[512,768]{1,0:T(8,128)(2,1)} %x.1), channel_id=1, source_target_pairs={{0,1},{1,2},{2,3},{4,5},{5,6},{6,7},{8,9},{9,10},{10,11},{12,13},{... | collective-permute-start | bytes 2359304 | tf_op jit(solution)/shard_map/ppermute | solution.py:806
  97.3 11.4 %copy-start.2 = (bf16[32,96,768]{2,1,0:T(8,128)(2,1)S(1)}, bf16[32,96,768]{2,1,0:T(8,128)(2,1)}, u32[]{:S(2)}) copy-start(bf16[32,96,768]{2,1,0:T(8,128)(2,1)} %get-tuple-element.73) | copy-start | bytes 14155780
  100.6 15.5 %collective-permute-start.8 = (bf16[16,24,3072]{2,1,0:T(8,128)(2,1)}, bf16[16,24,3072]{2,1,0:T(8,128)(2,1)}, u32[]{:S(2)}, u32[]{:S(2)}) collective-permute-start(bf16[16,24,3072]{2,1,0:T(8,128)(2,1)} %slice.46), channel_id=1, source_target_pairs={{0,1},{1,0},{2,3},{3,2},{4,5},{5,4},{6,7},{7,6},{8,9},{9,8},{10,11... | collective-permute-start | bytes 7077896 | tf_op jit(solution)/shard_map/ppermute | solution.py:753
  108.7 1.6 copy-start.7
  108.7 19.6 %slice-start = ((s8[4718592]{0:T(1024)(128)(4,1)}), s8[524288]{0:T(1024)(128)(4,1)S(1)}, s32[]{:S(2)}) async-start(s8[4718592]{0:T(1024)(128)(4,1)} %bitcast.19), calls=%async_computation | async-start | bytes 1048576
  110.2 15.6 %collective-permute-start.6 = (bf16[16,96,768]{2,1,0:T(8,128)(2,1)}, bf16[16,96,768]{2,1,0:T(8,128)(2,1)S(1)}, u32[]{:S(2)}, u32[]{:S(2)}) collective-permute-start(bf16[16,96,768]{2,1,0:T(8,128)(2,1)} %slice.43), channel_id=1, source_target_pairs={{0,1},{1,0},{2,3},{3,2},{4,5},{5,4},{6,7},{7,6},{8,9},{9,8},{10,11... | collective-permute-start | bytes 7077896 | tf_op jit(solution)/shard_map/ppermute | solution.py:753
  110.2 20.5 %collective-permute-start.5 = (f32[6,4,512]{2,1,0:T(4,128)S(1)}, f32[6,4,512]{2,1,0:T(4,128)S(1)}, u32[]{:S(2)}, u32[]{:S(2)}) collective-permute-start(f32[6,4,512]{2,1,0:T(4,128)S(1)} %copy-done.7), channel_id=1, source_target_pairs={{1,0},{2,1},{3,2},{5,4},{6,5},{7,6},{9,8},{10,9},{11,10},{13,12},{... | collective-permute-start | bytes 147464 | tf_op jit(solution)/shard_map/ppermute | solution.py:849
  111.5 19.3 %collective-permute-start.4 = (f32[6,4,512]{2,1,0:T(4,128)S(1)}, f32[6,4,512]{2,1,0:T(4,128)S(1)}, u32[]{:S(2)}, u32[]{:S(2)}) collective-permute-start(f32[6,4,512]{2,1,0:T(4,128)S(1)} %copy-done.7), channel_id=1, source_target_pairs={{0,1},{1,2},{2,3},{4,5},{5,6},{6,7},{8,9},{9,10},{10,11},{12,13},{... | collective-permute-start | bytes 147464 | tf_op jit(solution)/shard_map/ppermute | solution.py:848
  114.5 13.7 %slice-start.1 = ((s8[4718592]{0:T(1024)(128)(4,1)}), s8[4194304]{0:T(1024)(128)(4,1)S(1)}, s32[]{:S(2)}) async-start(s8[4718592]{0:T(1024)(128)(4,1)} %bitcast.19), calls=%async_computation.1 | async-start | bytes 8388608
  114.6 16.2 %collective-permute-start.3 = (bf16[512,768]{1,0:T(8,128)(2,1)}, bf16[512,768]{1,0:T(8,128)(2,1)}, u32[]{:S(2)}, u32[]{:S(2)}) collective-permute-start(bf16[512,768]{1,0:T(8,128)(2,1)} %get-tuple-element.61.go), channel_id=1, source_target_pairs={{1,0},{2,1},{3,2},{5,4},{6,5},{7,6},{9,8},{10,9},{11,10},{13,12},{... | collective-permute-start | bytes 2359304 | tf_op jit(solution)/shard_map/ppermute | solution.py:847
  116.1 14.7 %collective-permute-start.2 = (bf16[512,768]{1,0:T(8,128)(2,1)}, bf16[512,768]{1,0:T(8,128)(2,1)}, u32[]{:S(2)}, u32[]{:S(2)}) collective-permute-start(bf16[512,768]{1,0:T(8,128)(2,1)} %get-tuple-element.61.go), channel_id=1, source_target_pairs={{0,1},{1,2},{2,3},{4,5},{5,6},{6,7},{8,9},{9,10},{10,11},{12,13},{... | collective-permute-start | bytes 2359304 | tf_op jit(solution)/shard_map/ppermute | solution.py:846
  124.6 6.0 %copy-start = (bf16[16,24,3072]{2,1,0:T(8,128)(2,1)}, bf16[16,24,3072]{2,1,0:T(8,128)(2,1)S(1)}, u32[]{:S(2)}) copy-start(bf16[16,24,3072]{2,1,0:T(8,128)(2,1)S(1)} %add_convert_fusion.up_keep) | copy-start | bytes 7077892
  125.8 1.5 copy-start.3
  127.3 41.8 %collective-permute-start.9 = (bf16[8,24,3072]{2,1,0:T(8,128)(2,1)}, bf16[8,24,3072]{2,1,0:T(8,128)(2,1)}, u32[]{:S(2)}, u32[]{:S(2)}) collective-permute-start(bf16[8,24,3072]{2,1,0:T(8,128)(2,1)} %slice.57), channel_id=1, source_target_pairs={{0,2},{1,3},{2,0},{3,1},{4,6},{5,7},{6,4},{7,5},{8,10},{9,11},{10,... | collective-permute-start | bytes 3538952 | tf_op jit(solution)/shard_map/ppermute | solution.py:753
  130.6 38.5 %copy-start.1 = (bf16[16,96,768]{2,1,0:T(8,128)(2,1)}, bf16[16,96,768]{2,1,0:T(8,128)(2,1)S(1)}, u32[]{:S(2)}) copy-start(bf16[16,96,768]{2,1,0:T(8,128)(2,1)S(1)} %add_convert_fusion.1.dn_keep) | copy-start | bytes 7077892
  130.7 0.7 copy-start.8
  130.7 38.4 %collective-permute-start.7 = (bf16[8,96,768]{2,1,0:T(8,128)(2,1)S(1)}, bf16[8,96,768]{2,1,0:T(8,128)(2,1)S(1)}, u32[]{:S(2)}, u32[]{:S(2)}) collective-permute-start(bf16[8,96,768]{2,1,0:T(8,128)(2,1)S(1)} %slice.56), channel_id=1, source_target_pairs={{0,4},{1,5},{2,6},{3,7},{4,0},{5,1},{6,2},{7,3},{8,12},{9,13},{10,... | collective-permute-start | bytes 3538952 | tf_op jit(solution)/shard_map/ppermute | solution.py:753
  130.8 0.8 copy-start.9
  169.1 1.0 copy-start.6
  254.8 10.8 %copy-start.5 = (f32[24,3072]{1,0:T(8,128)S(1)}, f32[24,3072]{1,0:T(8,128)}, u32[]{:S(2)}) copy-start(f32[24,3072]{1,0:T(8,128)} %get-tuple-element.129) | copy-start | bytes 884740
  254.8 11.5 %copy-start.4 = (f32[96,768]{1,0:T(8,128)S(1)}, f32[96,768]{1,0:T(8,128)}, u32[]{:S(2)}) copy-start(f32[96,768]{1,0:T(8,128)} %get-tuple-element.131) | copy-start | bytes 884740
